TPU v7x, 32 devices: a whole 2x2x4 slice. The times are simulated.
32 devices in a mesh: space: 16 (over z, y, core), band: 2 (over x).
Axes of the slice: x: 2, y: 2, z: 4, core: 2. Of those that a mesh axis runs over, the one named last changes fastest.
Arguments:
- orbitals: float32 [48, 16, 8, 16, 128], P('band', 'space'), may hold values from -100 to 100
- potential: float32 [16, 8, 16, 128], P('space'), may hold values from 0.5 to 4
Outputs:
- basis: float32 [48, 16, 8, 16, 128], P('band', 'space')
- factor: float32 [48, 48], replicated
All inputs are finite; a program needn't handle non-finite values.
Results may differ from a plain program's by a relative error of at most 0.0003.
Values sent between devices are 32-bit elements; how exact they have to be, the bound alone decides.
A program may use at most 64 MiB of HBM per device.

v0:
```python
import jax
import jax.numpy as jnp
from jax import lax
from jax.sharding import PartitionSpec as P

DEG = 4


coefficients = (-205.0 / 72.0, 8.0 / 5.0, -1.0 / 5.0, 8.0 / 315.0, -1.0 / 560.0)
centre_value = 9.25
half_range = 4.75
filter_scale = 1.0 / 32.0


def shifted(block, axis, distance):
    devices = range(lax.axis_size(axis))
    route = [(i - distance, i) for i in devices if i - distance in devices]
    return lax.ppermute(block, axis, route)


def padded_along(field_in, axis_dim, stride, tile_count, coordinate):
    extent = field_in.shape[axis_dim]
    if tile_count == 1:
        widths = [(0, 0)] * field_in.ndim
        widths[axis_dim] = (4, 4)
        return jnp.pad(field_in, widths)
    top_layers = lax.slice_in_dim(field_in, extent - 4, extent, axis=axis_dim)
    bottom_layers = lax.slice_in_dim(field_in, 0, 4, axis=axis_dim)
    received = []
    for direction, portion, retain in (
        (1, top_layers, coordinate > 0),
        (-1, bottom_layers, coordinate < tile_count - 1),
    ):
        arrived = shifted(portion, "space", direction * stride)
        received.append(jnp.where(retain, arrived, jnp.zeros_like(arrived)))
    return jnp.concatenate([received[0], field_in, received[1]], axis=axis_dim)


def hamiltonian(field_in, potential, layout):
    total = 3.0 * coefficients[0] * field_in
    for axis_dim, stride, tile_count, coordinate in layout:
        padded = padded_along(field_in, axis_dim, stride, tile_count, coordinate)
        extent = field_in.shape[axis_dim]
        for offset in range(1, 5):
            upper = lax.slice_in_dim(padded, 4 + offset, 4 + offset + extent, axis=axis_dim)
            lower = lax.slice_in_dim(padded, 4 - offset, 4 - offset + extent, axis=axis_dim)
            total = total + coefficients[offset] * (upper + lower)
    return -0.5 * total + potential * field_in


def orthonormalize(flat, reduce_gram, total_cells, rows, own_count):
    count_orbs = flat.shape[0]
    identity = jnp.eye(count_orbs, dtype=jnp.float32)
    current = flat
    lowers = []
    for round_index in range(2):
        partial_gram = jnp.dot(
            current, current.T, precision=lax.Precision.HIGHEST, preferred_element_type=jnp.float32
        )
        gram = reduce_gram(partial_gram) / total_cells
        lower = jnp.linalg.cholesky(gram)
        inverse = jax.scipy.linalg.solve_triangular(lower, identity, lower=True)
        if round_index == 1:
            inverse = lax.dynamic_slice_in_dim(inverse, rows, own_count, axis=0)
        current = jnp.dot(
            inverse, current, precision=lax.Precision.HIGHEST, preferred_element_type=jnp.float32
        )
        lowers.append(lower)
    factor = jnp.dot(
        lowers[0], lowers[1], precision=lax.Precision.HIGHEST, preferred_element_type=jnp.float32
    ).T
    return (current, factor)


def shards(orbitals, potential):
    tile_index = lax.axis_index("space")
    layout = (
        (2, 16, lax.axis_size("space") // 16, tile_index // 16),
        (3, 4, 4, tile_index // 4 % 4),
        (4, 1, 4, tile_index % 4),
    )
    previous = orbitals
    current = (hamiltonian(orbitals, potential, layout) - centre_value * orbitals) / half_range
    for step_index in range(DEG - 1):
        following = (
            2.0 * (hamiltonian(current, potential, layout) - centre_value * current) / half_range
            - previous
        )
        previous, current = (current, following)
    filtered = current * filter_scale
    own_count = filtered.shape[0]
    everything = lax.all_gather(filtered, "band", axis=0, tiled=True)
    flat = everything.reshape(everything.shape[0], -1)
    total_cells = flat.shape[1] * lax.axis_size("space")

    def reduce_everywhere(partial_gram):
        total = partial_gram
        size = lax.axis_size("space")
        step = 1
        while step < size:
            route = [(i, i ^ step) for i in range(size)]
            total = total + lax.ppermute(total, "space", route)
            step *= 2
        return total

    rows = lax.axis_index("band") * own_count
    ortho, factor = orthonormalize(flat, reduce_everywhere, total_cells, rows, own_count)
    basis = ortho.reshape(filtered.shape)
    return (basis, factor)


def solution(mesh):
    return jax.shard_map(
        shards,
        mesh=mesh,
        in_specs=(P("band", "space", None, None, None), P("space", None, None, None)),
        out_specs=(P("band", "space", None, None, None), P()),
        check_vma=False,
    )
```

profile of v0, /device:TPU:0, one launch (start us, length us, event | category | flops | bytes accessed | tf_op | source)
XLA Modules:
  0.0 283.8 jit_solution(6056905545931784123)
XLA Ops:
  7.2 3.6 %fusion.249 = (f32[24,1,8,16,4]{4,3,2,1,0:T(8,128)S(1)}, f32[24,1,8,16,4]{4,3,2,1,0:T(8,128)}) fusion(f32[24,1,8,16,128]{4,3,2,1,0:T(8,128)} %param.5), kind=kLoop, calls=%fused_computation.417 | loop fusion | bytes 196608 | tf_op jit(solution)/shard_map/slice | solution.py:28
  10.8 3.1 %copy.136 = f32[24,1,8,16,4]{0,3,4,2,1:T(8,128)} copy(f32[24,1,8,16,4]{4,3,2,1,0:T(8,128)} %get-tuple-element.29) | data formatting | bytes 98304
  13.9 3.1 %collective-permute-start.3 = (f32[24,1,8,16,4]{0,3,4,2,1:T(8,128)}, f32[24,1,8,16,4]{0,3,4,2,1:T(8,128)}, u32[]{:S(2)}, u32[]{:S(2)}) collective-permute-start(f32[24,1,8,16,4]{0,3,4,2,1:T(8,128)} %copy.136), channel_id=1, source_target_pairs={{0,2},{2,4},{4,6},{6,8},{8,10},{10,12},{12,14},{14,16},{16,18},{18... | collective-permute-start | bytes 147464 | tf_op jit(solution)/shard_map/ppermute | solution.py:18
  18.0 1.3 collective-permute-start.2
  21.5 7.8 %collective-permute-start.1 = (f32[24,1,8,4,128]{4,0,3,2,1:T(8,128)S(1)}, f32[24,1,8,4,128]{4,0,3,2,1:T(8,128)}, u32[]{:S(2)}, u32[]{:S(2)}) collective-permute-start(f32[24,1,8,4,128]{4,0,3,2,1:T(8,128)S(1)} %get-tuple-element.27), channel_id=1, source_target_pairs={{0,8},{2,10},{4,12},{6,14},{8,16},{10,18},{12,20},{14,22},{16,24},... | collective-permute-start | bytes 1179656 | tf_op jit(solution)/shard_map/ppermute | solution.py:18
  29.2 1.3 collective-permute-start
  30.6 2.0 copy.106
  33.6 2.0 copy.104
  36.0 4.8 %collective-permute-done = f32[24,1,8,4,128]{4,0,3,2,1:T(8,128)S(1)} collective-permute-done((f32[24,1,8,4,128]{4,0,3,2,1:T(8,128)S(1)}, f32[24,1,8,4,128]{4,0,3,2,1:T(8,128)S(1)}, u32[]{:S(2)}, u32[]{:S(2)}) %collective-permute-start) | collective-permute-done | bytes 393248 | tf_op jit(solution)/shard_map/ppermute | solution.py:18
  40.9 9.5 %broadcast_multiply_fusion = (f32[24,1,8,16,128]{4,0,3,2,1:T(8,128)S(1)}, f32[24,1,8,16,128]{4,0,3,2,1:T(8,128)}) fusion(f32[24,1,8,16,128]{4,0,3,2,1:T(8,128)S(1)} %copy-done.5, f32[8,16,128]{2,1,0:T(8,128)S(1)} %bitcast.46, f32[24,1,8,16,4]{4,0,3,2,1:T(8,128)S(1)} %copy-done.7, f32[24,1,8,16,4]{4,0,3,2,1:T(8,128)} %copy.104, ...), kind=kLoop, calls=%fused_computation.359 | loop fusion | flops 23199744 | bytes 5668864 | tf_op jit(solution)/shard_map/div | solution.py:83
  50.4 1.7 fusion.246
  52.1 2.3 copy.112
  54.4 2.0 collective-permute-start.7
  57.4 3.5 %collective-permute-start.5 = (f32[24,1,8,4,128]{4,0,3,2,1:T(8,128)}, f32[24,1,8,4,128]{4,0,3,2,1:T(8,128)}, u32[]{:S(2)}, u32[]{:S(2)}) collective-permute-start(f32[24,1,8,4,128]{4,0,3,2,1:T(8,128)} %get-tuple-element.25), channel_id=1, source_target_pairs={{0,8},{2,10},{4,12},{6,14},{8,16},{10,18},{12,20},{14,22},{16,24},... | collective-permute-start | bytes 1179656 | tf_op jit(solution)/shard_map/ppermute | solution.py:18
  60.8 1.3 collective-permute-start.4
  62.1 1.6 copy.110
  63.7 1.5 collective-permute-start.6
  65.3 2.0 copy.113
  68.2 2.0 copy.111
  70.2 4.4 %collective-permute-done.4 = f32[24,1,8,4,128]{4,0,3,2,1:T(8,128)} collective-permute-done((f32[24,1,8,4,128]{4,0,3,2,1:T(8,128)}, f32[24,1,8,4,128]{4,0,3,2,1:T(8,128)}, u32[]{:S(2)}, u32[]{:S(2)}) %collective-permute-start.4) | collective-permute-done | bytes 393248 | tf_op jit(solution)/shard_map/ppermute | solution.py:18
  75.7 10.0 %fusion.66 = f32[24,1,8,16,128]{4,0,3,2,1:T(8,128)S(1)} fusion(f32[24,1,8,16,128]{4,0,3,2,1:T(8,128)S(1)} %get-tuple-element.12, f32[24,1,8,4,128]{4,0,3,2,1:T(8,128)S(1)} %broadcast_select_fusion.4, f32[24,1,8,4,128]{4,0,3,2,1:T(8,128)S(1)} %broadcast_select_fusion.5, f32[24,1,8,16,4]{4,0,3,2,1:T(8,128)} %copy.113, f32[24,1,8,16,4]{4,0,3,2,1:T(8,128)} %copy.111, ...), kind=kLoop, calls=%fused_computation.194 | loop fusion | flops 23592960 | bytes 7241728 | tf_op jit(solution)/shard_map/sub | solution.py:86
  85.7 1.7 fusion.244
  87.4 2.3 copy.117
  89.7 3.8 %collective-permute-start.11 = (f32[24,1,8,16,4]{0,3,4,2,1:T(8,128)S(1)}, f32[24,1,8,16,4]{0,3,4,2,1:T(8,128)}, u32[]{:S(2)}, u32[]{:S(2)}) collective-permute-start(f32[24,1,8,16,4]{0,3,4,2,1:T(8,128)S(1)} %copy.117), channel_id=1, source_target_pairs={{0,2},{2,4},{4,6},{6,8},{8,10},{10,12},{12,14},{14,16},{16,18},{18... | collective-permute-start | bytes 147464 | tf_op jit(solution)/shard_map/ppermute | solution.py:18
  94.5 6.7 %collective-permute-start.9 = (f32[24,1,8,4,128]{4,0,3,2,1:T(8,128)}, f32[24,1,8,4,128]{4,0,3,2,1:T(8,128)}, u32[]{:S(2)}, u32[]{:S(2)}) collective-permute-start(f32[24,1,8,4,128]{4,0,3,2,1:T(8,128)} %get-tuple-element.21), channel_id=1, source_target_pairs={{0,8},{2,10},{4,12},{6,14},{8,16},{10,18},{12,20},{14,22},{16,24},... | collective-permute-start | bytes 1179656 | tf_op jit(solution)/shard_map/ppermute | solution.py:18
  101.2 1.3 collective-permute-start.8
  102.5 1.6 copy.115
  105.4 2.0 copy.118
  107.7 2.0 copy.116
  109.7 2.7 collective-permute-done.8
  113.5 9.7 %fusion.41 = f32[24,1,8,16,128]{4,0,3,2,1:T(8,128)S(1)} fusion(f32[24,1,8,16,128]{4,0,3,2,1:T(8,128)S(1)} %fusion.66, f32[24,1,8,4,128]{4,0,3,2,1:T(8,128)S(1)} %broadcast_select_fusion.2, f32[24,1,8,4,128]{4,0,3,2,1:T(8,128)S(1)} %broadcast_select_fusion.3, f32[24,1,8,16,4]{4,0,3,2,1:T(8,128)} %copy.118, f32[24,1,8,16,4]{4,0,3,2,1:T(8,128)} %copy.116, ...), kind=kLoop, calls=%fused_computation.169 | loop fusion | flops 23986176 | bytes 5668864 | tf_op jit(solution)/shard_map/sub | solution.py:86
  123.2 2.2 fusion.242
  125.4 2.3 copy.121
  127.7 5.4 %collective-permute-start.15 = (f32[24,1,8,16,4]{0,3,4,2,1:T(8,128)S(1)}, f32[24,1,8,16,4]{0,3,4,2,1:T(8,128)}, u32[]{:S(2)}, u32[]{:S(2)}) collective-permute-start(f32[24,1,8,16,4]{0,3,4,2,1:T(8,128)S(1)} %copy.121), channel_id=1, source_target_pairs={{0,2},{2,4},{4,6},{6,8},{8,10},{10,12},{12,14},{14,16},{16,18},{18... | collective-permute-start | bytes 147464 | tf_op jit(solution)/shard_map/ppermute | solution.py:18
  134.1 5.3 %collective-permute-start.13 = (f32[24,1,8,4,128]{4,0,3,2,1:T(8,128)}, f32[24,1,8,4,128]{4,0,3,2,1:T(8,128)}, u32[]{:S(2)}, u32[]{:S(2)}) collective-permute-start(f32[24,1,8,4,128]{4,0,3,2,1:T(8,128)} %get-tuple-element.17), channel_id=1, source_target_pairs={{0,8},{2,10},{4,12},{6,14},{8,16},{10,18},{12,20},{14,22},{16,24},... | collective-permute-start | bytes 1179656 | tf_op jit(solution)/shard_map/ppermute | solution.py:18
  140.6 3.0 %copy.119 = f32[24,1,8,16,4]{0,3,4,2,1:T(8,128)} copy(f32[24,1,8,16,4]{4,0,3,2,1:T(8,128)} %get-tuple-element.14) | data formatting | bytes 98304 | tf_op jit(solution)/shard_map/slice | solution.py:28
  143.6 1.5 collective-permute-start.14
  145.2 2.0 copy.122
  148.4 2.0 copy.120
  150.4 1.9 collective-permute-done.12
  153.3 9.4 %fusion.16 = f32[24,1,8,16,128]{4,0,3,2,1:T(8,128)} fusion(f32[24,1,8,16,128]{4,0,3,2,1:T(8,128)S(1)} %fusion.66, f32[24,1,8,16,128]{4,0,3,2,1:T(8,128)S(1)} %fusion.41, f32[24,1,8,4,128]{4,0,3,2,1:T(8,128)S(1)} %broadcast_select_fusion, f32[24,1,8,4,128]{4,0,3,2,1:T(8,128)S(1)} %broadcast_select_fusion.1, f32[24,1,8,16,4]{4,0,3,2,1:T(8,128)S(1)} %copy-done.6, ...), kind=kLoop, calls=%fused_computation.144 | loop fusion | flops 23986176 | bytes 5668864 | tf_op jit(solution)/shard_map/mul | solution.py:90
  162.7 48.3 %all-gather.2.cloned.1.call-done = f32[48,1,8,16,128]{4,0,3,2,1:T(8,128)} async-done(((f32[24,1,8,16,128]{4,0,3,2,1:T(8,128)}), f32[48,1,8,16,128]{4,0,3,2,1:T(8,128)}) %all-gather.2.cloned.1.call-update) | async-done | bytes 3145744 | tf_op jit(solution)/shard_map/all_gather | solution.py:92
  211.1 5.6 %fusion.213 = f32[48,48]{0,1:T(8,128)S(1)} fusion(f32[48,1,8,16,128]{4,0,3,2,1:T(8,128)} %all-gather.2.cloned.1.call-done), kind=kOutput, calls=%fused_computation.358 | convolution fusion | flops 452984832 | bytes 3154944 | tf_op jit(solution)/shard_map/dot_general | solution.py:57
  217.9 1.5 collective-permute-start.17
  219.4 2.4 collective-permute-done.17
  221.8 1.5 collective-permute-start.18
  223.3 2.3 collective-permute-done.18
  225.6 2.4 collective-permute-start.19
  229.0 2.4 reshape.26
  231.5 4.4 %cholesky.44 = f32[48,48]{1,0:T(8,128)S(1)} custom-call(f32[48,48]{1,0:T(8,128)S(1)} %fusion.223), custom_call_target="Cholesky" | custom-call | tf_op jit(solution)/shard_map/jit(cholesky)/cholesky | solution.py:61
  237.2 3.7 %custom-call.6 = f32[1,48,48]{1,2,0:T(8,128)S(1)} custom-call(f32[1,48,48]{2,1,0:T(8,128)S(1)} %fusion.227), custom_call_target="InvertDiagBlocksLowerTriangular" | custom-call | tf_op jit(solution)/shard_map/jit(_solve_triangular)/triangular_solve | solution.py:62
  241.1 4.6 %fusion.250 = f32[48,16384]{1,0:T(8,128)S(1)} fusion(f32[48,48]{1,0:T(8,128)S(1)} %fusion.218, f32[48,16384]{1,0:T(8,128)} %reshape.26), kind=kOutput, calls=%fused_computation.418 | convolution fusion | flops 452984832 | bytes 6300672 | tf_op jit(solution)/shard_map/dot_general | solution.py:65
  245.8 2.6 fusion.251
  249.6 1.5 collective-permute-start.21
  251.1 2.3 collective-permute-done.21
  253.5 1.5 collective-permute-start.22
  254.9 2.3 collective-permute-done.22
  257.3 1.4 collective-permute-start.23
  258.7 3.4 %collective-permute-done.23 = f32[48,48]{0,1:T(8,128)S(1)} collective-permute-done((f32[48,48]{0,1:T(8,128)S(1)}, f32[48,48]{0,1:T(8,128)S(1)}, u32[]{:S(2)}, u32[]{:S(2)}) %collective-permute-start.23) | collective-permute-done | bytes 9248 | tf_op jit(solution)/shard_map/ppermute | solution.py:102
  262.1 4.4 %cholesky.55 = f32[48,48]{1,0:T(8,128)S(1)} custom-call(f32[48,48]{1,0:T(8,128)S(1)} %fusion.221), custom_call_target="Cholesky" | custom-call | tf_op jit(solution)/shard_map/jit(cholesky)/cholesky | solution.py:61
  267.9 2.1 fusion.230
  270.0 3.7 %custom-call.7 = f32[1,48,48]{1,2,0:T(8,128)S(1)} custom-call(f32[1,48,48]{2,1,0:T(8,128)S(1)} %select_bitcast_fusion), custom_call_target="InvertDiagBlocksLowerTriangular" | custom-call | tf_op jit(solution)/shard_map/jit(_solve_triangular)/triangular_solve | solution.py:62
  273.9 1.6 convolution_bitcast_fusion
  275.6 1.4 copy.137
  (83 shorter events, 22.7 us)
Async XLA Ops:
  7.2 203.9 %all-gather.2.cloned.1.call-start = ((), (), s32[]{:S(2)}) async-start(), calls=%async_computation | async-start | bytes 4718592 | tf_op jit(solution)/shard_map/all_gather | solution.py:92
  10.8 8.5 %copy-start = (f32[24,1,8,16,128]{4,3,2,1,0:T(8,128)S(1)}, f32[24,1,8,16,128]{4,3,2,1,0:T(8,128)}, u32[]{:S(2)}) copy-start(f32[24,1,8,16,128]{4,3,2,1,0:T(8,128)} %param.5) | copy-start | bytes 4718596
  13.9 16.6 %collective-permute-start.3 = (f32[24,1,8,16,4]{0,3,4,2,1:T(8,128)}, f32[24,1,8,16,4]{0,3,4,2,1:T(8,128)}, u32[]{:S(2)}, u32[]{:S(2)}) collective-permute-start(f32[24,1,8,16,4]{0,3,4,2,1:T(8,128)} %copy.136), channel_id=1, source_target_pairs={{0,2},{2,4},{4,6},{6,8},{8,10},{10,12},{12,14},{14,16},{16,18},{18... | collective-permute-start | bytes 147464 | tf_op jit(solution)/shard_map/ppermute | solution.py:18
  18.0 14.6 %collective-permute-start.2 = (f32[24,1,8,16,4]{0,3,4,2,1:T(8,128)S(1)}, f32[24,1,8,16,4]{0,3,4,2,1:T(8,128)}, u32[]{:S(2)}, u32[]{:S(2)}) collective-permute-start(f32[24,1,8,16,4]{0,3,4,2,1:T(8,128)S(1)} %copy.135), channel_id=1, source_target_pairs={{2,0},{4,2},{6,4},{8,6},{10,8},{12,10},{14,12},{16,14},{18,16},{20... | collective-permute-start | bytes 147464 | tf_op jit(solution)/shard_map/ppermute | solution.py:18
  20.2 1.1 copy-start.4
  21.4 9.1 %copy-start.8 = (f32[1,8,16,128]{3,2,1,0:T(8,128)S(1)}, f32[1,8,16,128]{3,2,1,0:T(8,128)}, u32[]{:S(2)}) copy-start(f32[1,8,16,128]{3,2,1,0:T(8,128)} %param.6) | copy-start | bytes 196612
  21.5 14.6 %collective-permute-start.1 = (f32[24,1,8,4,128]{4,0,3,2,1:T(8,128)S(1)}, f32[24,1,8,4,128]{4,0,3,2,1:T(8,128)}, u32[]{:S(2)}, u32[]{:S(2)}) collective-permute-start(f32[24,1,8,4,128]{4,0,3,2,1:T(8,128)S(1)} %get-tuple-element.27), channel_id=1, source_target_pairs={{0,8},{2,10},{4,12},{6,14},{8,16},{10,18},{12,20},{14,22},{16,24},... | collective-permute-start | bytes 1179656 | tf_op jit(solution)/shard_map/ppermute | solution.py:18
  29.2 11.6 %collective-permute-start = (f32[24,1,8,4,128]{4,0,3,2,1:T(8,128)S(1)}, f32[24,1,8,4,128]{4,0,3,2,1:T(8,128)S(1)}, u32[]{:S(2)}, u32[]{:S(2)}) collective-permute-start(f32[24,1,8,4,128]{4,0,3,2,1:T(8,128)S(1)} %get-tuple-element.26), channel_id=1, source_target_pairs={{8,0},{10,2},{12,4},{14,6},{16,8},{18,10},{20,12},{22,14},{24,16},... | collective-permute-start | bytes 1179656 | tf_op jit(solution)/shard_map/ppermute | solution.py:18
  33.6 7.3 %copy-start.5 = (f32[24,1,8,16,128]{4,0,3,2,1:T(8,128)S(1)}, f32[24,1,8,16,128]{4,0,3,2,1:T(8,128)}, u32[]{:S(2)}) copy-start(f32[24,1,8,16,128]{4,0,3,2,1:T(8,128)} %copy-done.4) | copy-start | bytes 4718596
  35.6 5.3 %copy-start.7 = (f32[24,1,8,16,4]{4,0,3,2,1:T(8,128)S(1)}, f32[24,1,8,16,4]{4,0,3,2,1:T(8,128)}, u32[]{:S(2)}) copy-start(f32[24,1,8,16,4]{4,0,3,2,1:T(8,128)} %copy.106) | copy-start | bytes 147460
  54.4 10.8 %collective-permute-start.7 = (f32[24,1,8,16,4]{0,3,4,2,1:T(8,128)S(1)}, f32[24,1,8,16,4]{0,3,4,2,1:T(8,128)}, u32[]{:S(2)}, u32[]{:S(2)}) collective-permute-start(f32[24,1,8,16,4]{0,3,4,2,1:T(8,128)S(1)} %copy.112), channel_id=1, source_target_pairs={{0,2},{2,4},{4,6},{6,8},{8,10},{10,12},{12,14},{14,16},{16,18},{18... | collective-permute-start | bytes 147464 | tf_op jit(solution)/shard_map/ppermute | solution.py:18
  57.4 12.8 %collective-permute-start.5 = (f32[24,1,8,4,128]{4,0,3,2,1:T(8,128)}, f32[24,1,8,4,128]{4,0,3,2,1:T(8,128)}, u32[]{:S(2)}, u32[]{:S(2)}) collective-permute-start(f32[24,1,8,4,128]{4,0,3,2,1:T(8,128)} %get-tuple-element.25), channel_id=1, source_target_pairs={{0,8},{2,10},{4,12},{6,14},{8,16},{10,18},{12,20},{14,22},{16,24},... | collective-permute-start | bytes 1179656 | tf_op jit(solution)/shard_map/ppermute | solution.py:18
  60.8 13.8 %collective-permute-start.4 = (f32[24,1,8,4,128]{4,0,3,2,1:T(8,128)}, f32[24,1,8,4,128]{4,0,3,2,1:T(8,128)}, u32[]{:S(2)}, u32[]{:S(2)}) collective-permute-start(f32[24,1,8,4,128]{4,0,3,2,1:T(8,128)} %get-tuple-element.24), channel_id=1, source_target_pairs={{8,0},{10,2},{12,4},{14,6},{16,8},{18,10},{20,12},{22,14},{24,16},... | collective-permute-start | bytes 1179656 | tf_op jit(solution)/shard_map/ppermute | solution.py:18
  63.7 4.5 %collective-permute-start.6 = (f32[24,1,8,16,4]{0,3,4,2,1:T(8,128)}, f32[24,1,8,16,4]{0,3,4,2,1:T(8,128)S(1)}, u32[]{:S(2)}, u32[]{:S(2)}) collective-permute-start(f32[24,1,8,16,4]{0,3,4,2,1:T(8,128)} %copy.110), channel_id=1, source_target_pairs={{2,0},{4,2},{6,4},{8,6},{10,8},{12,10},{14,12},{16,14},{18,16},{20... | collective-permute-start | bytes 147464 | tf_op jit(solution)/shard_map/ppermute | solution.py:18
  70.2 5.5 %copy-start.1 = (f32[24,1,8,16,128]{4,3,2,1,0:T(8,128)S(1)}, f32[24,1,8,16,128]{4,3,2,1,0:T(8,128)}, u32[]{:S(2)}) copy-start(f32[24,1,8,16,128]{4,3,2,1,0:T(8,128)} %param.5) | copy-start | bytes 4718596
  89.7 15.6 %collective-permute-start.11 = (f32[24,1,8,16,4]{0,3,4,2,1:T(8,128)S(1)}, f32[24,1,8,16,4]{0,3,4,2,1:T(8,128)}, u32[]{:S(2)}, u32[]{:S(2)}) collective-permute-start(f32[24,1,8,16,4]{0,3,4,2,1:T(8,128)S(1)} %copy.117), channel_id=1, source_target_pairs={{0,2},{2,4},{4,6},{6,8},{8,10},{10,12},{12,14},{14,16},{16,18},{18... | collective-permute-start | bytes 147464 | tf_op jit(solution)/shard_map/ppermute | solution.py:18
  94.5 15.2 %collective-permute-start.9 = (f32[24,1,8,4,128]{4,0,3,2,1:T(8,128)}, f32[24,1,8,4,128]{4,0,3,2,1:T(8,128)}, u32[]{:S(2)}, u32[]{:S(2)}) collective-permute-start(f32[24,1,8,4,128]{4,0,3,2,1:T(8,128)} %get-tuple-element.21), channel_id=1, source_target_pairs={{0,8},{2,10},{4,12},{6,14},{8,16},{10,18},{12,20},{14,22},{16,24},... | collective-permute-start | bytes 1179656 | tf_op jit(solution)/shard_map/ppermute | solution.py:18
  101.2 11.3 %collective-permute-start.8 = (f32[24,1,8,4,128]{4,0,3,2,1:T(8,128)}, f32[24,1,8,4,128]{4,0,3,2,1:T(8,128)}, u32[]{:S(2)}, u32[]{:S(2)}) collective-permute-start(f32[24,1,8,4,128]{4,0,3,2,1:T(8,128)} %get-tuple-element.20), channel_id=1, source_target_pairs={{8,0},{10,2},{12,4},{14,6},{16,8},{18,10},{20,12},{22,14},{24,16},... | collective-permute-start | bytes 1179656 | tf_op jit(solution)/shard_map/ppermute | solution.py:18
  104.1 3.6 %collective-permute-start.10 = (f32[24,1,8,16,4]{0,3,4,2,1:T(8,128)}, f32[24,1,8,16,4]{0,3,4,2,1:T(8,128)S(1)}, u32[]{:S(2)}, u32[]{:S(2)}) collective-permute-start(f32[24,1,8,16,4]{0,3,4,2,1:T(8,128)} %copy.115), channel_id=1, source_target_pairs={{2,0},{4,2},{6,4},{8,6},{10,8},{12,10},{14,12},{16,14},{18,16},{20... | collective-permute-start | bytes 147464 | tf_op jit(solution)/shard_map/ppermute | solution.py:18
  109.7 3.8 %copy-start.2 = (f32[24,1,8,16,128]{4,0,3,2,1:T(8,128)S(1)}, f32[24,1,8,16,128]{4,0,3,2,1:T(8,128)}, u32[]{:S(2)}) copy-start(f32[24,1,8,16,128]{4,0,3,2,1:T(8,128)} %get-tuple-element.13) | copy-start | bytes 4718596
  127.7 17.4 %collective-permute-start.15 = (f32[24,1,8,16,4]{0,3,4,2,1:T(8,128)S(1)}, f32[24,1,8,16,4]{0,3,4,2,1:T(8,128)}, u32[]{:S(2)}, u32[]{:S(2)}) collective-permute-start(f32[24,1,8,16,4]{0,3,4,2,1:T(8,128)S(1)} %copy.121), channel_id=1, source_target_pairs={{0,2},{2,4},{4,6},{6,8},{8,10},{10,12},{12,14},{14,16},{16,18},{18... | collective-permute-start | bytes 147464 | tf_op jit(solution)/shard_map/ppermute | solution.py:18
  134.1 16.3 %collective-permute-start.13 = (f32[24,1,8,4,128]{4,0,3,2,1:T(8,128)}, f32[24,1,8,4,128]{4,0,3,2,1:T(8,128)}, u32[]{:S(2)}, u32[]{:S(2)}) collective-permute-start(f32[24,1,8,4,128]{4,0,3,2,1:T(8,128)} %get-tuple-element.17), channel_id=1, source_target_pairs={{0,8},{2,10},{4,12},{6,14},{8,16},{10,18},{12,20},{14,22},{16,24},... | collective-permute-start | bytes 1179656 | tf_op jit(solution)/shard_map/ppermute | solution.py:18
  139.3 13.0 %collective-permute-start.12 = (f32[24,1,8,4,128]{4,0,3,2,1:T(8,128)}, f32[24,1,8,4,128]{4,0,3,2,1:T(8,128)}, u32[]{:S(2)}, u32[]{:S(2)}) collective-permute-start(f32[24,1,8,4,128]{4,0,3,2,1:T(8,128)} %get-tuple-element.16), channel_id=1, source_target_pairs={{8,0},{10,2},{12,4},{14,6},{16,8},{18,10},{20,12},{22,14},{24,16},... | collective-permute-start | bytes 1179656 | tf_op jit(solution)/shard_map/ppermute | solution.py:18
  143.6 3.8 %collective-permute-start.14 = (f32[24,1,8,16,4]{0,3,4,2,1:T(8,128)}, f32[24,1,8,16,4]{0,3,4,2,1:T(8,128)}, u32[]{:S(2)}, u32[]{:S(2)}) collective-permute-start(f32[24,1,8,16,4]{0,3,4,2,1:T(8,128)} %copy.119), channel_id=1, source_target_pairs={{2,0},{4,2},{6,4},{8,6},{10,8},{12,10},{14,12},{16,14},{18,16},{20... | collective-permute-start | bytes 147464 | tf_op jit(solution)/shard_map/ppermute | solution.py:18
  150.4 2.9 %copy-start.6 = (f32[24,1,8,16,4]{4,0,3,2,1:T(8,128)S(1)}, f32[24,1,8,16,4]{4,0,3,2,1:T(8,128)}, u32[]{:S(2)}) copy-start(f32[24,1,8,16,4]{4,0,3,2,1:T(8,128)} %copy.122) | copy-start | bytes 147460
  211.1 17.0 %copy-start.3 = (f32[48,1,8,16,128]{4,0,3,2,1:T(8,128)S(1)}, f32[48,1,8,16,128]{4,0,3,2,1:T(8,128)}, u32[]{:S(2)}) copy-start(f32[48,1,8,16,128]{4,0,3,2,1:T(8,128)} %all-gather.2.cloned.1.call-done) | copy-start | bytes 9437188
  216.7 1.3 collective-permute-start.16
  217.9 3.8 %collective-permute-start.17 = (f32[48,48]{0,1:T(8,128)S(1)}, f32[48,48]{0,1:T(8,128)S(1)}, u32[]{:S(2)}, u32[]{:S(2)}) collective-permute-start(f32[48,48]{0,1:T(8,128)S(1)} %add.454), channel_id=1, source_target_pairs={{0,4},{2,6},{4,0},{6,2},{8,12},{10,14},{12,8},{14,10},{16,20},{18,... | collective-permute-start | bytes 27656 | tf_op jit(solution)/shard_map/ppermute | solution.py:102
  221.8 3.8 %collective-permute-start.18 = (f32[48,48]{0,1:T(8,128)S(1)}, f32[48,48]{0,1:T(8,128)S(1)}, u32[]{:S(2)}, u32[]{:S(2)}) collective-permute-start(f32[48,48]{0,1:T(8,128)S(1)} %add.455), channel_id=1, source_target_pairs={{0,8},{2,10},{4,12},{6,14},{8,0},{10,2},{12,4},{14,6},{16,24},{18,... | collective-permute-start | bytes 27656 | tf_op jit(solution)/shard_map/ppermute | solution.py:102
  225.6 5.8 %collective-permute-start.19 = (f32[48,48]{0,1:T(8,128)S(1)}, f32[48,48]{0,1:T(8,128)S(1)}, u32[]{:S(2)}, u32[]{:S(2)}) collective-permute-start(f32[48,48]{0,1:T(8,128)S(1)} %add.456), channel_id=1, source_target_pairs={{0,16},{2,18},{4,20},{6,22},{8,24},{10,26},{12,28},{14,30},{16,0},... | collective-permute-start | bytes 27656 | tf_op jit(solution)/shard_map/ppermute | solution.py:102
  248.4 1.3 collective-permute-start.20
  249.6 3.8 %collective-permute-start.21 = (f32[48,48]{0,1:T(8,128)S(1)}, f32[48,48]{0,1:T(8,128)S(1)}, u32[]{:S(2)}, u32[]{:S(2)}) collective-permute-start(f32[48,48]{0,1:T(8,128)S(1)} %add.458), channel_id=1, source_target_pairs={{0,4},{2,6},{4,0},{6,2},{8,12},{10,14},{12,8},{14,10},{16,20},{18,... | collective-permute-start | bytes 27656 | tf_op jit(solution)/shard_map/ppermute | solution.py:102
  253.5 3.8 %collective-permute-start.22 = (f32[48,48]{0,1:T(8,128)S(1)}, f32[48,48]{0,1:T(8,128)S(1)}, u32[]{:S(2)}, u32[]{:S(2)}) collective-permute-start(f32[48,48]{0,1:T(8,128)S(1)} %add.459), channel_id=1, source_target_pairs={{0,8},{2,10},{4,12},{6,14},{8,0},{10,2},{12,4},{14,6},{16,24},{18,... | collective-permute-start | bytes 27656 | tf_op jit(solution)/shard_map/ppermute | solution.py:102
  257.3 4.7 %collective-permute-start.23 = (f32[48,48]{0,1:T(8,128)S(1)}, f32[48,48]{0,1:T(8,128)S(1)}, u32[]{:S(2)}, u32[]{:S(2)}) collective-permute-start(f32[48,48]{0,1:T(8,128)S(1)} %add.460), channel_id=1, source_target_pairs={{0,16},{2,18},{4,20},{6,22},{8,24},{10,26},{12,28},{14,30},{16,0},... | collective-permute-start | bytes 27656 | tf_op jit(solution)/shard_map/ppermute | solution.py:102
Sparse Core Ops, SparseCore 0:
  162.8 48.1 all-gather.1
where the time goes:
time: 285 us; the launch traced here: 284 us
  waiting for transfers between devices  79.2 us (28%)
  other arithmetic  62.8 us (22%)
  starting transfers between devices  58 us (20%)
  local copies, waits for them, and re-layouts  52.3 us (18%)
  matrix products  17 us (6%)
  between operations  14.5 us (5%)
    all_gather x1, waiting for transfers between devices, shards(): everything = lax.all_gather(filtered, 'band', axis=0, tiled=True)  48.3 us
    ppermute x16, starting transfers between devices, shifted(): return lax.ppermute(block, axis, route)  48.1 us
    sub x2, other arithmetic, shards(): 2.0 * (hamiltonian(current, potential, layout) - centre_value * current)  19.7 us
    slice x11, local copies, waits for them, and re-layouts, padded_along(): bottom_layers = lax.slice_in_dim(field_in, 0, 4, axis=axis_dim)  18.4 us
    select_n x8, local copies, waits for them, and re-layouts, padded_along(): received.append(jnp.where(retain, arrived, jnp.zeros_like(arrived)))  15.9 us
    ppermute x16, waiting for transfers between devices, shifted(): return lax.ppermute(block, axis, route)  15.7 us
    ppermute x8, waiting for transfers between devices, reduce_everywhere(): total = total + lax.ppermute(total, 'space', route)  15.1 us
    another operation x6, other arithmetic, orthonormalize(): lower = jnp.linalg.cholesky(gram)  10.2 us
  transfers between devices with their start and end apart: 25, of which 16 were waited for; matrix products, arithmetic and copies ran while one was open for 11% of the time, Pallas kernels for 0%

commit v1 on v0

--- a/solution.py
+++ b/solution.py
@@ -89,7 +89,14 @@
         previous, current = (current, following)
     filtered = current * filter_scale
     own_count = filtered.shape[0]
-    everything = lax.all_gather(filtered, "band", axis=0, tiled=True)
+    if lax.axis_size("band") == 2:
+        other = lax.ppermute(filtered, "band", [(0, 1), (1, 0)])
+        first_band = lax.axis_index("band") == 0
+        everything = jnp.concatenate(
+            [jnp.where(first_band, filtered, other), jnp.where(first_band, other, filtered)], axis=0
+        )
+    else:
+        everything = lax.all_gather(filtered, "band", axis=0, tiled=True)
     flat = everything.reshape(everything.shape[0], -1)
     total_cells = flat.shape[1] * lax.axis_size("space")
 

time: 285 us -> 263 us (0.923)
  waiting for transfers between devices: 79.2 us -> 63.2 us
  between operations: 14.5 us -> 1.13 us
  starting transfers between devices: 58 us -> 65.2 us
  matrix products: 17 us -> 14.1 us
    all_gather x1 -> x0, waiting for transfers between devices: 48.3 us -> none  [shards(): everything = lax.all_gather(filtered, 'band', axis=0, tiled=True)]
    ppermute x0 -> x1, waiting for transfers between devices: none -> 33.5 us  [shards(): other = lax.ppermute(filtered, 'band', [(0, 1), (1, 0)])]
    ppermute x8, starting transfers between devices: 9.84 us -> 15.5 us  [reduce_everywhere(): total = total + lax.ppermute(total, 'space', route)]
    dot_general x2, matrix products: 8.18 us -> 5.16 us  [orthonormalize(): jnp.dot(current, current.T, precision=lax.Precision.HIGHEST, preferred_el...]
    unnamed x22 -> x20, local copies, waits for them, and re-layouts: 7.59 us -> 7.58 us
  transfers between devices with their start and end apart: 25 -> 25, of which waited for: 16 -> 17; matrix products, arithmetic and copies ran while one was open for 11% -> 13% of each run, Pallas kernels for 0% -> 0%
where the time goes in v1:
time: 263 us; the launch traced here: 262 us
  other arithmetic  65.5 us (25%)
  starting transfers between devices  65.2 us (25%)
  waiting for transfers between devices  63.2 us (24%)
  local copies, waits for them, and re-layouts  52.5 us (20%)
  matrix products  14.1 us (5%)
    ppermute x16, starting transfers between devices, shifted(): return lax.ppermute(block, axis, route)  48.2 us
    ppermute x1, waiting for transfers between devices, shards(): other = lax.ppermute(filtered, 'band', [(0, 1), (1, 0)])  33.5 us
    sub x2, other arithmetic, shards(): 2.0 * (hamiltonian(current, potential, layout) - centre_value * current)  20.3 us
    slice x11, local copies, waits for them, and re-layouts, padded_along(): bottom_layers = lax.slice_in_dim(field_in, 0, 4, axis=axis_dim)  18.5 us
    select_n x8, local copies, waits for them, and re-layouts, padded_along(): received.append(jnp.where(retain, arrived, jnp.zeros_like(arrived)))  16 us
    ppermute x16, waiting for transfers between devices, shifted(): return lax.ppermute(block, axis, route)  15.6 us
    ppermute x8, starting transfers between devices, reduce_everywhere(): total = total + lax.ppermute(total, 'space', route)  15.5 us
    ppermute x8, waiting for transfers between devices, reduce_everywhere(): total = total + lax.ppermute(total, 'space', route)  14.1 us
  transfers between devices with their start and end apart: 25, of which 17 were waited for; matrix products, arithmetic and copies ran while one was open for 13% of the time, Pallas kernels for 0%

profile of v1, /device:TPU:0, one launch (start us, length us, event | category | flops | bytes accessed | tf_op | source)
XLA Modules:
  0.0 261.6 jit_solution(16374565535647163960)
XLA Ops:
  0.6 3.7 %fusion.249 = (f32[24,1,8,16,4]{4,3,2,1,0:T(8,128)S(1)}, f32[24,1,8,16,4]{4,3,2,1,0:T(8,128)}) fusion(f32[24,1,8,16,128]{4,3,2,1,0:T(8,128)} %param.5), kind=kLoop, calls=%fused_computation.420 | loop fusion | bytes 196608 | tf_op jit(solution)/shard_map/slice | solution.py:28
  4.3 3.1 %copy.136 = f32[24,1,8,16,4]{0,3,4,2,1:T(8,128)} copy(f32[24,1,8,16,4]{4,3,2,1,0:T(8,128)} %get-tuple-element.31) | data formatting | bytes 98304
  7.4 3.1 %collective-permute-start.3 = (f32[24,1,8,16,4]{0,3,4,2,1:T(8,128)}, f32[24,1,8,16,4]{0,3,4,2,1:T(8,128)}, u32[]{:S(2)}, u32[]{:S(2)}) collective-permute-start(f32[24,1,8,16,4]{0,3,4,2,1:T(8,128)} %copy.136), channel_id=1, source_target_pairs={{0,2},{2,4},{4,6},{6,8},{8,10},{10,12},{12,14},{14,16},{16,18},{18... | collective-permute-start | bytes 147464 | tf_op jit(solution)/shard_map/ppermute | solution.py:18
  11.5 1.3 collective-permute-start.2
  14.9 7.8 %collective-permute-start.1 = (f32[24,1,8,4,128]{4,0,3,2,1:T(8,128)S(1)}, f32[24,1,8,4,128]{4,0,3,2,1:T(8,128)}, u32[]{:S(2)}, u32[]{:S(2)}) collective-permute-start(f32[24,1,8,4,128]{4,0,3,2,1:T(8,128)S(1)} %get-tuple-element.29), channel_id=1, source_target_pairs={{0,8},{2,10},{4,12},{6,14},{8,16},{10,18},{12,20},{14,22},{16,24},... | collective-permute-start | bytes 1179656 | tf_op jit(solution)/shard_map/ppermute | solution.py:18
  22.7 1.3 collective-permute-start
  24.1 2.0 copy.106
  27.1 2.0 copy.104
  29.5 4.8 %collective-permute-done = f32[24,1,8,4,128]{4,0,3,2,1:T(8,128)S(1)} collective-permute-done((f32[24,1,8,4,128]{4,0,3,2,1:T(8,128)S(1)}, f32[24,1,8,4,128]{4,0,3,2,1:T(8,128)S(1)}, u32[]{:S(2)}, u32[]{:S(2)}) %collective-permute-start) | collective-permute-done | bytes 393248 | tf_op jit(solution)/shard_map/ppermute | solution.py:18
  34.4 9.6 %broadcast_multiply_fusion = (f32[24,1,8,16,128]{4,0,3,2,1:T(8,128)S(1)}, f32[24,1,8,16,128]{4,0,3,2,1:T(8,128)}) fusion(f32[24,1,8,16,128]{4,0,3,2,1:T(8,128)S(1)} %copy-done.4, f32[8,16,128]{2,1,0:T(8,128)S(1)} %bitcast.46, f32[24,1,8,16,4]{4,0,3,2,1:T(8,128)S(1)} %copy-done.6, f32[24,1,8,16,4]{4,0,3,2,1:T(8,128)} %copy.104, ...), kind=kLoop, calls=%fused_computation.360 | loop fusion | flops 23199744 | bytes 5668864 | tf_op jit(solution)/shard_map/div | solution.py:83
  44.0 1.7 fusion.246
  45.7 2.3 copy.112
  48.0 2.0 collective-permute-start.7
  50.9 3.5 %collective-permute-start.5 = (f32[24,1,8,4,128]{4,0,3,2,1:T(8,128)}, f32[24,1,8,4,128]{4,0,3,2,1:T(8,128)}, u32[]{:S(2)}, u32[]{:S(2)}) collective-permute-start(f32[24,1,8,4,128]{4,0,3,2,1:T(8,128)} %get-tuple-element.27), channel_id=1, source_target_pairs={{0,8},{2,10},{4,12},{6,14},{8,16},{10,18},{12,20},{14,22},{16,24},... | collective-permute-start | bytes 1179656 | tf_op jit(solution)/shard_map/ppermute | solution.py:18
  54.4 1.3 collective-permute-start.4
  55.7 1.6 copy.110
  57.3 1.5 collective-permute-start.6
  58.8 2.0 copy.113
  61.8 2.0 copy.111
  63.8 4.4 %collective-permute-done.4 = f32[24,1,8,4,128]{4,0,3,2,1:T(8,128)} collective-permute-done((f32[24,1,8,4,128]{4,0,3,2,1:T(8,128)}, f32[24,1,8,4,128]{4,0,3,2,1:T(8,128)}, u32[]{:S(2)}, u32[]{:S(2)}) %collective-permute-start.4) | collective-permute-done | bytes 393248 | tf_op jit(solution)/shard_map/ppermute | solution.py:18
  69.2 10.3 %fusion.66 = f32[24,1,8,16,128]{4,0,3,2,1:T(8,128)S(1)} fusion(f32[24,1,8,16,128]{4,0,3,2,1:T(8,128)S(1)} %get-tuple-element.12, f32[24,1,8,4,128]{4,0,3,2,1:T(8,128)S(1)} %broadcast_select_fusion.6, f32[24,1,8,4,128]{4,0,3,2,1:T(8,128)S(1)} %broadcast_select_fusion.7, f32[24,1,8,16,4]{4,0,3,2,1:T(8,128)} %copy.113, f32[24,1,8,16,4]{4,0,3,2,1:T(8,128)} %copy.111, ...), kind=kLoop, calls=%fused_computation.195 | loop fusion | flops 23592960 | bytes 7241728 | tf_op jit(solution)/shard_map/sub | solution.py:86
  79.6 1.7 fusion.244
  81.3 2.3 copy.117
  83.6 3.8 %collective-permute-start.11 = (f32[24,1,8,16,4]{0,3,4,2,1:T(8,128)S(1)}, f32[24,1,8,16,4]{0,3,4,2,1:T(8,128)}, u32[]{:S(2)}, u32[]{:S(2)}) collective-permute-start(f32[24,1,8,16,4]{0,3,4,2,1:T(8,128)S(1)} %copy.117), channel_id=1, source_target_pairs={{0,2},{2,4},{4,6},{6,8},{8,10},{10,12},{12,14},{14,16},{16,18},{18... | collective-permute-start | bytes 147464 | tf_op jit(solution)/shard_map/ppermute | solution.py:18
  88.3 6.7 %collective-permute-start.9 = (f32[24,1,8,4,128]{4,0,3,2,1:T(8,128)}, f32[24,1,8,4,128]{4,0,3,2,1:T(8,128)}, u32[]{:S(2)}, u32[]{:S(2)}) collective-permute-start(f32[24,1,8,4,128]{4,0,3,2,1:T(8,128)} %get-tuple-element.23), channel_id=1, source_target_pairs={{0,8},{2,10},{4,12},{6,14},{8,16},{10,18},{12,20},{14,22},{16,24},... | collective-permute-start | bytes 1179656 | tf_op jit(solution)/shard_map/ppermute | solution.py:18
  96.3 1.6 copy.115
  99.3 2.0 copy.118
  101.6 2.0 copy.116
  103.6 2.7 %collective-permute-done.8 = f32[24,1,8,4,128]{4,0,3,2,1:T(8,128)} collective-permute-done((f32[24,1,8,4,128]{4,0,3,2,1:T(8,128)}, f32[24,1,8,4,128]{4,0,3,2,1:T(8,128)}, u32[]{:S(2)}, u32[]{:S(2)}) %collective-permute-start.8) | collective-permute-done | bytes 393248 | tf_op jit(solution)/shard_map/ppermute | solution.py:18
  107.4 9.9 %fusion.41 = f32[24,1,8,16,128]{4,0,3,2,1:T(8,128)S(1)} fusion(f32[24,1,8,16,128]{4,0,3,2,1:T(8,128)S(1)} %fusion.66, f32[24,1,8,4,128]{4,0,3,2,1:T(8,128)S(1)} %broadcast_select_fusion.4, f32[24,1,8,4,128]{4,0,3,2,1:T(8,128)S(1)} %broadcast_select_fusion.5, f32[24,1,8,16,4]{4,0,3,2,1:T(8,128)} %copy.118, f32[24,1,8,16,4]{4,0,3,2,1:T(8,128)} %copy.116, ...), kind=kLoop, calls=%fused_computation.170 | loop fusion | flops 23986176 | bytes 5668864 | tf_op jit(solution)/shard_map/sub | solution.py:86
  117.3 2.2 fusion.242
  119.5 2.3 copy.121
  121.8 5.4 %collective-permute-start.15 = (f32[24,1,8,16,4]{0,3,4,2,1:T(8,128)S(1)}, f32[24,1,8,16,4]{0,3,4,2,1:T(8,128)}, u32[]{:S(2)}, u32[]{:S(2)}) collective-permute-start(f32[24,1,8,16,4]{0,3,4,2,1:T(8,128)S(1)} %copy.121), channel_id=1, source_target_pairs={{0,2},{2,4},{4,6},{6,8},{8,10},{10,12},{12,14},{14,16},{16,18},{18... | collective-permute-start | bytes 147464 | tf_op jit(solution)/shard_map/ppermute | solution.py:18
  128.2 5.3 %collective-permute-start.13 = (f32[24,1,8,4,128]{4,0,3,2,1:T(8,128)}, f32[24,1,8,4,128]{4,0,3,2,1:T(8,128)}, u32[]{:S(2)}, u32[]{:S(2)}) collective-permute-start(f32[24,1,8,4,128]{4,0,3,2,1:T(8,128)} %get-tuple-element.19), channel_id=1, source_target_pairs={{0,8},{2,10},{4,12},{6,14},{8,16},{10,18},{12,20},{14,22},{16,24},... | collective-permute-start | bytes 1179656 | tf_op jit(solution)/shard_map/ppermute | solution.py:18
  134.8 3.0 %copy.119 = f32[24,1,8,16,4]{0,3,4,2,1:T(8,128)} copy(f32[24,1,8,16,4]{4,0,3,2,1:T(8,128)} %get-tuple-element.16) | data formatting | bytes 98304 | tf_op jit(solution)/shard_map/slice | solution.py:28
  137.8 1.5 collective-permute-start.14
  139.3 2.0 copy.122
  142.5 2.0 copy.120
  144.6 1.9 collective-permute-done.12
  147.5 9.5 %fusion.16 = f32[24,1,8,16,128]{4,0,3,2,1:T(8,128)} fusion(f32[24,1,8,16,128]{4,0,3,2,1:T(8,128)S(1)} %fusion.66, f32[24,1,8,16,128]{4,0,3,2,1:T(8,128)S(1)} %fusion.41, f32[24,1,8,4,128]{4,0,3,2,1:T(8,128)S(1)} %broadcast_select_fusion.2, f32[24,1,8,4,128]{4,0,3,2,1:T(8,128)S(1)} %broadcast_select_fusion.3, f32[24,1,8,16,4]{4,0,3,2,1:T(8,128)S(1)} %copy-done.5, ...), kind=kLoop, calls=%fused_computation.145 | loop fusion | flops 23986176 | bytes 5668864 | tf_op jit(solution)/shard_map/mul | solution.py:90
  157.0 1.5 collective-permute-start.16
  158.4 33.5 %collective-permute-done.16 = f32[24,1,8,16,128]{4,0,3,2,1:T(8,128)S(1)} collective-permute-done((f32[24,1,8,16,128]{4,0,3,2,1:T(8,128)}, f32[24,1,8,16,128]{4,0,3,2,1:T(8,128)S(1)}, u32[]{:S(2)}, u32[]{:S(2)}) %collective-permute-start.16) | collective-permute-done | bytes 1572896 | tf_op jit(solution)/shard_map/ppermute | solution.py:93
  191.9 1.7 broadcast_select_fusion.1
  193.6 2.6 fusion.213
  196.2 2.4 collective-permute-start.17
  199.4 2.9 %collective-permute-start.18 = (f32[48,48]{0,1:T(8,128)S(1)}, f32[48,48]{0,1:T(8,128)S(1)}, u32[]{:S(2)}, u32[]{:S(2)}) collective-permute-start(f32[48,48]{0,1:T(8,128)S(1)} %add.454), channel_id=1, source_target_pairs={{0,4},{2,6},{4,0},{6,2},{8,12},{10,14},{12,8},{14,10},{16,20},{18,... | collective-permute-start | bytes 27656 | tf_op jit(solution)/shard_map/ppermute | solution.py:109
  202.3 1.8 collective-permute-done.18
  204.1 5.2 %collective-permute-start.19 = (f32[48,48]{0,1:T(8,128)S(1)}, f32[48,48]{0,1:T(8,128)S(1)}, u32[]{:S(2)}, u32[]{:S(2)}) collective-permute-start(f32[48,48]{0,1:T(8,128)S(1)} %add.455), channel_id=1, source_target_pairs={{0,8},{2,10},{4,12},{6,14},{8,0},{10,2},{12,4},{14,6},{16,24},{18,... | collective-permute-start | bytes 27656 | tf_op jit(solution)/shard_map/ppermute | solution.py:109
  209.3 1.8 collective-permute-done.19
  213.2 2.4 reshape.26
  216.0 4.4 %cholesky.44 = f32[48,48]{1,0:T(8,128)S(1)} custom-call(f32[48,48]{1,0:T(8,128)S(1)} %fusion.223), custom_call_target="Cholesky" | custom-call | tf_op jit(solution)/shard_map/jit(cholesky)/cholesky | solution.py:61
  221.7 3.7 %custom-call.6 = f32[1,48,48]{1,2,0:T(8,128)S(1)} custom-call(f32[1,48,48]{2,1,0:T(8,128)S(1)} %fusion.227), custom_call_target="InvertDiagBlocksLowerTriangular" | custom-call | tf_op jit(solution)/shard_map/jit(_solve_triangular)/triangular_solve | solution.py:62
  225.6 4.6 %fusion.250 = f32[48,16384]{1,0:T(8,128)S(1)} fusion(f32[48,48]{1,0:T(8,128)S(1)} %fusion.218, f32[48,16384]{1,0:T(8,128)} %reshape.26), kind=kOutput, calls=%fused_computation.421 | convolution fusion | flops 452984832 | bytes 6300672 | tf_op jit(solution)/shard_map/dot_general | solution.py:65
  230.2 2.6 fusion.251
  234.5 3.5 %collective-permute-done.22 = f32[48,48]{0,1:T(8,128)S(1)} collective-permute-done((f32[48,48]{0,1:T(8,128)S(1)}, f32[48,48]{0,1:T(8,128)S(1)}, u32[]{:S(2)}, u32[]{:S(2)}) %collective-permute-start.22) | collective-permute-done | bytes 9248 | tf_op jit(solution)/shard_map/ppermute | solution.py:109
  237.9 2.0 collective-permute-start.23
  240.0 1.8 collective-permute-done.23
  241.8 1.9 collective-permute-start.24
  243.6 2.9 %collective-permute-done.24 = f32[48,48]{0,1:T(8,128)S(1)} collective-permute-done((f32[48,48]{0,1:T(8,128)S(1)}, f32[48,48]{0,1:T(8,128)S(1)}, u32[]{:S(2)}, u32[]{:S(2)}) %collective-permute-start.24) | collective-permute-done | bytes 9248 | tf_op jit(solution)/shard_map/ppermute | solution.py:109
  246.6 4.4 %cholesky.55 = f32[48,48]{1,0:T(8,128)S(1)} custom-call(f32[48,48]{1,0:T(8,128)S(1)} %fusion.221), custom_call_target="Cholesky" | custom-call | tf_op jit(solution)/shard_map/jit(cholesky)/cholesky | solution.py:61
  252.4 2.2 fusion.230
  254.6 3.7 %custom-call.7 = f32[1,48,48]{1,2,0:T(8,128)S(1)} custom-call(f32[1,48,48]{2,1,0:T(8,128)S(1)} %select_bitcast_fusion), custom_call_target="InvertDiagBlocksLowerTriangular" | custom-call | tf_op jit(solution)/shard_map/jit(_solve_triangular)/triangular_solve | solution.py:62
  258.5 1.6 convolution_bitcast_fusion
  260.2 1.4 copy.137
  (82 shorter events, 25.2 us)
Async XLA Ops:
  4.3 8.5 %copy-start = (f32[24,1,8,16,128]{4,3,2,1,0:T(8,128)S(1)}, f32[24,1,8,16,128]{4,3,2,1,0:T(8,128)}, u32[]{:S(2)}) copy-start(f32[24,1,8,16,128]{4,3,2,1,0:T(8,128)} %param.5) | copy-start | bytes 4718596
  7.4 16.6 %collective-permute-start.3 = (f32[24,1,8,16,4]{0,3,4,2,1:T(8,128)}, f32[24,1,8,16,4]{0,3,4,2,1:T(8,128)}, u32[]{:S(2)}, u32[]{:S(2)}) collective-permute-start(f32[24,1,8,16,4]{0,3,4,2,1:T(8,128)} %copy.136), channel_id=1, source_target_pairs={{0,2},{2,4},{4,6},{6,8},{8,10},{10,12},{12,14},{14,16},{16,18},{18... | collective-permute-start | bytes 147464 | tf_op jit(solution)/shard_map/ppermute | solution.py:18
  11.5 14.6 %collective-permute-start.2 = (f32[24,1,8,16,4]{0,3,4,2,1:T(8,128)S(1)}, f32[24,1,8,16,4]{0,3,4,2,1:T(8,128)}, u32[]{:S(2)}, u32[]{:S(2)}) collective-permute-start(f32[24,1,8,16,4]{0,3,4,2,1:T(8,128)S(1)} %copy.135), channel_id=1, source_target_pairs={{2,0},{4,2},{6,4},{8,6},{10,8},{12,10},{14,12},{16,14},{18,16},{20... | collective-permute-start | bytes 147464 | tf_op jit(solution)/shard_map/ppermute | solution.py:18
  13.7 1.1 copy-start.3
  14.9 9.1 %copy-start.7 = (f32[1,8,16,128]{3,2,1,0:T(8,128)S(1)}, f32[1,8,16,128]{3,2,1,0:T(8,128)}, u32[]{:S(2)}) copy-start(f32[1,8,16,128]{3,2,1,0:T(8,128)} %param.6) | copy-start | bytes 196612
  14.9 14.6 %collective-permute-start.1 = (f32[24,1,8,4,128]{4,0,3,2,1:T(8,128)S(1)}, f32[24,1,8,4,128]{4,0,3,2,1:T(8,128)}, u32[]{:S(2)}, u32[]{:S(2)}) collective-permute-start(f32[24,1,8,4,128]{4,0,3,2,1:T(8,128)S(1)} %get-tuple-element.29), channel_id=1, source_target_pairs={{0,8},{2,10},{4,12},{6,14},{8,16},{10,18},{12,20},{14,22},{16,24},... | collective-permute-start | bytes 1179656 | tf_op jit(solution)/shard_map/ppermute | solution.py:18
  22.7 11.6 %collective-permute-start = (f32[24,1,8,4,128]{4,0,3,2,1:T(8,128)S(1)}, f32[24,1,8,4,128]{4,0,3,2,1:T(8,128)S(1)}, u32[]{:S(2)}, u32[]{:S(2)}) collective-permute-start(f32[24,1,8,4,128]{4,0,3,2,1:T(8,128)S(1)} %get-tuple-element.28), channel_id=1, source_target_pairs={{8,0},{10,2},{12,4},{14,6},{16,8},{18,10},{20,12},{22,14},{24,16},... | collective-permute-start | bytes 1179656 | tf_op jit(solution)/shard_map/ppermute | solution.py:18
  27.1 7.3 %copy-start.4 = (f32[24,1,8,16,128]{4,0,3,2,1:T(8,128)S(1)}, f32[24,1,8,16,128]{4,0,3,2,1:T(8,128)}, u32[]{:S(2)}) copy-start(f32[24,1,8,16,128]{4,0,3,2,1:T(8,128)} %copy-done.3) | copy-start | bytes 4718596
  29.1 5.3 %copy-start.6 = (f32[24,1,8,16,4]{4,0,3,2,1:T(8,128)S(1)}, f32[24,1,8,16,4]{4,0,3,2,1:T(8,128)}, u32[]{:S(2)}) copy-start(f32[24,1,8,16,4]{4,0,3,2,1:T(8,128)} %copy.106) | copy-start | bytes 147460
  48.0 10.8 %collective-permute-start.7 = (f32[24,1,8,16,4]{0,3,4,2,1:T(8,128)S(1)}, f32[24,1,8,16,4]{0,3,4,2,1:T(8,128)}, u32[]{:S(2)}, u32[]{:S(2)}) collective-permute-start(f32[24,1,8,16,4]{0,3,4,2,1:T(8,128)S(1)} %copy.112), channel_id=1, source_target_pairs={{0,2},{2,4},{4,6},{6,8},{8,10},{10,12},{12,14},{14,16},{16,18},{18... | collective-permute-start | bytes 147464 | tf_op jit(solution)/shard_map/ppermute | solution.py:18
  50.9 12.8 %collective-permute-start.5 = (f32[24,1,8,4,128]{4,0,3,2,1:T(8,128)}, f32[24,1,8,4,128]{4,0,3,2,1:T(8,128)}, u32[]{:S(2)}, u32[]{:S(2)}) collective-permute-start(f32[24,1,8,4,128]{4,0,3,2,1:T(8,128)} %get-tuple-element.27), channel_id=1, source_target_pairs={{0,8},{2,10},{4,12},{6,14},{8,16},{10,18},{12,20},{14,22},{16,24},... | collective-permute-start | bytes 1179656 | tf_op jit(solution)/shard_map/ppermute | solution.py:18
  54.4 13.8 %collective-permute-start.4 = (f32[24,1,8,4,128]{4,0,3,2,1:T(8,128)}, f32[24,1,8,4,128]{4,0,3,2,1:T(8,128)}, u32[]{:S(2)}, u32[]{:S(2)}) collective-permute-start(f32[24,1,8,4,128]{4,0,3,2,1:T(8,128)} %get-tuple-element.26), channel_id=1, source_target_pairs={{8,0},{10,2},{12,4},{14,6},{16,8},{18,10},{20,12},{22,14},{24,16},... | collective-permute-start | bytes 1179656 | tf_op jit(solution)/shard_map/ppermute | solution.py:18
  57.3 4.5 %collective-permute-start.6 = (f32[24,1,8,16,4]{0,3,4,2,1:T(8,128)}, f32[24,1,8,16,4]{0,3,4,2,1:T(8,128)S(1)}, u32[]{:S(2)}, u32[]{:S(2)}) collective-permute-start(f32[24,1,8,16,4]{0,3,4,2,1:T(8,128)} %copy.110), channel_id=1, source_target_pairs={{2,0},{4,2},{6,4},{8,6},{10,8},{12,10},{14,12},{16,14},{18,16},{20... | collective-permute-start | bytes 147464 | tf_op jit(solution)/shard_map/ppermute | solution.py:18
  63.8 5.5 %copy-start.1 = (f32[24,1,8,16,128]{4,3,2,1,0:T(8,128)S(1)}, f32[24,1,8,16,128]{4,3,2,1,0:T(8,128)}, u32[]{:S(2)}) copy-start(f32[24,1,8,16,128]{4,3,2,1,0:T(8,128)} %param.5) | copy-start | bytes 4718596
  83.6 15.7 %collective-permute-start.11 = (f32[24,1,8,16,4]{0,3,4,2,1:T(8,128)S(1)}, f32[24,1,8,16,4]{0,3,4,2,1:T(8,128)}, u32[]{:S(2)}, u32[]{:S(2)}) collective-permute-start(f32[24,1,8,16,4]{0,3,4,2,1:T(8,128)S(1)} %copy.117), channel_id=1, source_target_pairs={{0,2},{2,4},{4,6},{6,8},{8,10},{10,12},{12,14},{14,16},{16,18},{18... | collective-permute-start | bytes 147464 | tf_op jit(solution)/shard_map/ppermute | solution.py:18
  88.3 15.2 %collective-permute-start.9 = (f32[24,1,8,4,128]{4,0,3,2,1:T(8,128)}, f32[24,1,8,4,128]{4,0,3,2,1:T(8,128)}, u32[]{:S(2)}, u32[]{:S(2)}) collective-permute-start(f32[24,1,8,4,128]{4,0,3,2,1:T(8,128)} %get-tuple-element.23), channel_id=1, source_target_pairs={{0,8},{2,10},{4,12},{6,14},{8,16},{10,18},{12,20},{14,22},{16,24},... | collective-permute-start | bytes 1179656 | tf_op jit(solution)/shard_map/ppermute | solution.py:18
  95.0 11.3 %collective-permute-start.8 = (f32[24,1,8,4,128]{4,0,3,2,1:T(8,128)}, f32[24,1,8,4,128]{4,0,3,2,1:T(8,128)}, u32[]{:S(2)}, u32[]{:S(2)}) collective-permute-start(f32[24,1,8,4,128]{4,0,3,2,1:T(8,128)} %get-tuple-element.22), channel_id=1, source_target_pairs={{8,0},{10,2},{12,4},{14,6},{16,8},{18,10},{20,12},{22,14},{24,16},... | collective-permute-start | bytes 1179656 | tf_op jit(solution)/shard_map/ppermute | solution.py:18
  97.9 3.6 %collective-permute-start.10 = (f32[24,1,8,16,4]{0,3,4,2,1:T(8,128)}, f32[24,1,8,16,4]{0,3,4,2,1:T(8,128)S(1)}, u32[]{:S(2)}, u32[]{:S(2)}) collective-permute-start(f32[24,1,8,16,4]{0,3,4,2,1:T(8,128)} %copy.115), channel_id=1, source_target_pairs={{2,0},{4,2},{6,4},{8,6},{10,8},{12,10},{14,12},{16,14},{18,16},{20... | collective-permute-start | bytes 147464 | tf_op jit(solution)/shard_map/ppermute | solution.py:18
  103.6 3.8 %copy-start.2 = (f32[24,1,8,16,128]{4,0,3,2,1:T(8,128)S(1)}, f32[24,1,8,16,128]{4,0,3,2,1:T(8,128)}, u32[]{:S(2)}) copy-start(f32[24,1,8,16,128]{4,0,3,2,1:T(8,128)} %get-tuple-element.13) | copy-start | bytes 4718596
  121.8 17.4 %collective-permute-start.15 = (f32[24,1,8,16,4]{0,3,4,2,1:T(8,128)S(1)}, f32[24,1,8,16,4]{0,3,4,2,1:T(8,128)}, u32[]{:S(2)}, u32[]{:S(2)}) collective-permute-start(f32[24,1,8,16,4]{0,3,4,2,1:T(8,128)S(1)} %copy.121), channel_id=1, source_target_pairs={{0,2},{2,4},{4,6},{6,8},{8,10},{10,12},{12,14},{14,16},{16,18},{18... | collective-permute-start | bytes 147464 | tf_op jit(solution)/shard_map/ppermute | solution.py:18
  128.2 16.4 %collective-permute-start.13 = (f32[24,1,8,4,128]{4,0,3,2,1:T(8,128)}, f32[24,1,8,4,128]{4,0,3,2,1:T(8,128)}, u32[]{:S(2)}, u32[]{:S(2)}) collective-permute-start(f32[24,1,8,4,128]{4,0,3,2,1:T(8,128)} %get-tuple-element.19), channel_id=1, source_target_pairs={{0,8},{2,10},{4,12},{6,14},{8,16},{10,18},{12,20},{14,22},{16,24},... | collective-permute-start | bytes 1179656 | tf_op jit(solution)/shard_map/ppermute | solution.py:18
  133.5 13.0 %collective-permute-start.12 = (f32[24,1,8,4,128]{4,0,3,2,1:T(8,128)}, f32[24,1,8,4,128]{4,0,3,2,1:T(8,128)}, u32[]{:S(2)}, u32[]{:S(2)}) collective-permute-start(f32[24,1,8,4,128]{4,0,3,2,1:T(8,128)} %get-tuple-element.18), channel_id=1, source_target_pairs={{8,0},{10,2},{12,4},{14,6},{16,8},{18,10},{20,12},{22,14},{24,16},... | collective-permute-start | bytes 1179656 | tf_op jit(solution)/shard_map/ppermute | solution.py:18
  137.8 3.8 %collective-permute-start.14 = (f32[24,1,8,16,4]{0,3,4,2,1:T(8,128)}, f32[24,1,8,16,4]{0,3,4,2,1:T(8,128)}, u32[]{:S(2)}, u32[]{:S(2)}) collective-permute-start(f32[24,1,8,16,4]{0,3,4,2,1:T(8,128)} %copy.119), channel_id=1, source_target_pairs={{2,0},{4,2},{6,4},{8,6},{10,8},{12,10},{14,12},{16,14},{18,16},{20... | collective-permute-start | bytes 147464 | tf_op jit(solution)/shard_map/ppermute | solution.py:18
  144.5 2.9 %copy-start.5 = (f32[24,1,8,16,4]{4,0,3,2,1:T(8,128)S(1)}, f32[24,1,8,16,4]{4,0,3,2,1:T(8,128)}, u32[]{:S(2)}) copy-start(f32[24,1,8,16,4]{4,0,3,2,1:T(8,128)} %copy.122) | copy-start | bytes 147460
  157.0 35.0 %collective-permute-start.16 = (f32[24,1,8,16,128]{4,0,3,2,1:T(8,128)}, f32[24,1,8,16,128]{4,0,3,2,1:T(8,128)S(1)}, u32[]{:S(2)}, u32[]{:S(2)}) collective-permute-start(f32[24,1,8,16,128]{4,0,3,2,1:T(8,128)} %fusion.16), channel_id=1, source_target_pairs={{0,1},{1,0},{2,3},{3,2},{4,5},{5,4},{6,7},{7,6},{8,9},{9,8},{10,11... | collective-permute-start | bytes 4718600 | tf_op jit(solution)/shard_map/ppermute | solution.py:93
  196.2 3.2 %collective-permute-start.17 = (f32[48,48]{0,1:T(8,128)S(1)}, f32[48,48]{0,1:T(8,128)S(1)}, u32[]{:S(2)}, u32[]{:S(2)}) collective-permute-start(f32[48,48]{0,1:T(8,128)S(1)} %fusion.213), channel_id=1, source_target_pairs={{0,2},{2,0},{4,6},{6,4},{8,10},{10,8},{12,14},{14,12},{16,18},{18,... | collective-permute-start | bytes 27656 | tf_op jit(solution)/shard_map/ppermute | solution.py:109
  199.4 4.7 %collective-permute-start.18 = (f32[48,48]{0,1:T(8,128)S(1)}, f32[48,48]{0,1:T(8,128)S(1)}, u32[]{:S(2)}, u32[]{:S(2)}) collective-permute-start(f32[48,48]{0,1:T(8,128)S(1)} %add.454), channel_id=1, source_target_pairs={{0,4},{2,6},{4,0},{6,2},{8,12},{10,14},{12,8},{14,10},{16,20},{18,... | collective-permute-start | bytes 27656 | tf_op jit(solution)/shard_map/ppermute | solution.py:109
  204.1 7.0 %collective-permute-start.19 = (f32[48,48]{0,1:T(8,128)S(1)}, f32[48,48]{0,1:T(8,128)S(1)}, u32[]{:S(2)}, u32[]{:S(2)}) collective-permute-start(f32[48,48]{0,1:T(8,128)S(1)} %add.455), channel_id=1, source_target_pairs={{0,8},{2,10},{4,12},{6,14},{8,0},{10,2},{12,4},{14,6},{16,24},{18,... | collective-permute-start | bytes 27656 | tf_op jit(solution)/shard_map/ppermute | solution.py:109
  211.1 4.7 %collective-permute-start.20 = (f32[48,48]{0,1:T(8,128)S(1)}, f32[48,48]{0,1:T(8,128)S(1)}, u32[]{:S(2)}, u32[]{:S(2)}) collective-permute-start(f32[48,48]{0,1:T(8,128)S(1)} %add.456), channel_id=1, source_target_pairs={{0,16},{2,18},{4,20},{6,22},{8,24},{10,26},{12,28},{14,30},{16,0},... | collective-permute-start | bytes 27656 | tf_op jit(solution)/shard_map/ppermute | solution.py:109
  232.8 1.3 collective-permute-start.21
  234.1 3.8 %collective-permute-start.22 = (f32[48,48]{0,1:T(8,128)S(1)}, f32[48,48]{0,1:T(8,128)S(1)}, u32[]{:S(2)}, u32[]{:S(2)}) collective-permute-start(f32[48,48]{0,1:T(8,128)S(1)} %add.458), channel_id=1, source_target_pairs={{0,4},{2,6},{4,0},{6,2},{8,12},{10,14},{12,8},{14,10},{16,20},{18,... | collective-permute-start | bytes 27656 | tf_op jit(solution)/shard_map/ppermute | solution.py:109
  237.9 3.8 %collective-permute-start.23 = (f32[48,48]{0,1:T(8,128)S(1)}, f32[48,48]{0,1:T(8,128)S(1)}, u32[]{:S(2)}, u32[]{:S(2)}) collective-permute-start(f32[48,48]{0,1:T(8,128)S(1)} %add.459), channel_id=1, source_target_pairs={{0,8},{2,10},{4,12},{6,14},{8,0},{10,2},{12,4},{14,6},{16,24},{18,... | collective-permute-start | bytes 27656 | tf_op jit(solution)/shard_map/ppermute | solution.py:109
  241.8 4.7 %collective-permute-start.24 = (f32[48,48]{0,1:T(8,128)S(1)}, f32[48,48]{0,1:T(8,128)S(1)}, u32[]{:S(2)}, u32[]{:S(2)}) collective-permute-start(f32[48,48]{0,1:T(8,128)S(1)} %add.460), channel_id=1, source_target_pairs={{0,16},{2,18},{4,20},{6,22},{8,24},{10,26},{12,28},{14,30},{16,0},... | collective-permute-start | bytes 27656 | tf_op jit(solution)/shard_map/ppermute | solution.py:109

commit v2 on v1

--- a/solution.py
+++ b/solution.py
@@ -54,16 +54,17 @@
     current = flat
     lowers = []
     for round_index in range(2):
-        partial_gram = jnp.dot(
-            current, current.T, precision=lax.Precision.HIGHEST, preferred_element_type=jnp.float32
+        partial_gram = jnp.tensordot(
+            current, current, axes=(tuple(range(1, current.ndim)),) * 2,
+            precision=lax.Precision.HIGHEST, preferred_element_type=jnp.float32,
         )
         gram = reduce_gram(partial_gram) / total_cells
         lower = jnp.linalg.cholesky(gram)
         inverse = jax.scipy.linalg.solve_triangular(lower, identity, lower=True)
         if round_index == 1:
             inverse = lax.dynamic_slice_in_dim(inverse, rows, own_count, axis=0)
-        current = jnp.dot(
-            inverse, current, precision=lax.Precision.HIGHEST, preferred_element_type=jnp.float32
+        current = jnp.tensordot(
+            inverse, current, axes=1, precision=lax.Precision.HIGHEST, preferred_element_type=jnp.float32
         )
         lowers.append(lower)
     factor = jnp.dot(
@@ -97,8 +98,8 @@
         )
     else:
         everything = lax.all_gather(filtered, "band", axis=0, tiled=True)
-    flat = everything.reshape(everything.shape[0], -1)
-    total_cells = flat.shape[1] * lax.axis_size("space")
+    flat = everything
+    total_cells = everything[0].size * lax.axis_size("space")
 
     def reduce_everywhere(partial_gram):
         total = partial_gram

time: 263 us -> 256 us (0.973)
  waiting for transfers between devices: 63.2 us -> 56.8 us
  local copies, waits for them, and re-layouts: 52.5 us -> 48.3 us
  starting transfers between devices: 65.2 us -> 68.6 us
    ppermute x16, waiting for transfers between devices: 15.6 us -> 11.9 us  [shifted(): return lax.ppermute(block, axis, route)]
  transfers between devices with their start and end apart: 25 -> 25, of which waited for: 17 -> 14; matrix products, arithmetic and copies ran while one was open for 13% -> 14% of each run, Pallas kernels for 0% -> 0%
where the time goes in v2:
time: 256 us; the launch traced here: 255 us
  starting transfers between devices  68.6 us (27%)
  other arithmetic  66.1 us (26%)
  waiting for transfers between devices  56.8 us (22%)
  local copies, waits for them, and re-layouts  48.3 us (19%)
  matrix products  13.9 us (5%)
    ppermute x16, starting transfers between devices, shifted(): return lax.ppermute(block, axis, route)  50.1 us
    ppermute x1, waiting for transfers between devices, shards(): other = lax.ppermute(filtered, 'band', [(0, 1), (1, 0)])  31.7 us
    sub x2, other arithmetic, shards(): 2.0 * (hamiltonian(current, potential, layout) - centre_value * current)  20.4 us
    slice x11, local copies, waits for them, and re-layouts, padded_along(): bottom_layers = lax.slice_in_dim(field_in, 0, 4, axis=axis_dim)  18.7 us
    ppermute x8, starting transfers between devices, reduce_everywhere(): total = total + lax.ppermute(total, 'space', route)  17 us
    select_n x8, local copies, waits for them, and re-layouts, padded_along(): received.append(jnp.where(retain, arrived, jnp.zeros_like(arrived)))  15.8 us
    ppermute x8, waiting for transfers between devices, reduce_everywhere(): total = total + lax.ppermute(total, 'space', route)  13.2 us
    ppermute x16, waiting for transfers between devices, shifted(): return lax.ppermute(block, axis, route)  11.9 us
  transfers between devices with their start and end apart: 25, of which 14 were waited for; matrix products, arithmetic and copies ran while one was open for 14% of the time, Pallas kernels for 0%

profile of v2, /device:TPU:0, one launch (start us, length us, event | category | flops | bytes accessed | tf_op | source)
XLA Modules:
  0.0 254.8 jit_solution(16623714517147376939)
XLA Ops:
  0.6 2.3 copy.74
  3.9 5.7 %collective-permute-start.1 = (f32[24,1,8,4,128]{4,0,3,2,1:T(8,128)}, f32[24,1,8,4,128]{4,0,3,2,1:T(8,128)}, u32[]{:S(2)}, u32[]{:S(2)}) collective-permute-start(f32[24,1,8,4,128]{4,0,3,2,1:T(8,128)} %get-tuple-element.27), channel_id=1, source_target_pairs={{0,8},{2,10},{4,12},{6,14},{8,16},{10,18},{12,20},{14,22},{16,24},... | collective-permute-start | bytes 1179656 | tf_op jit(solution)/shard_map/ppermute | solution.py:18
  10.9 1.7 fusion.249
  12.6 3.0 %copy.116 = f32[24,1,8,16,4]{0,3,4,2,1:T(8,128)} copy(f32[24,1,8,16,4]{4,3,2,1,0:T(8,128)} %get-tuple-element.28) | data formatting | bytes 98304
  17.9 3.0 %collective-permute-start.3 = (f32[24,1,8,16,4]{0,3,4,2,1:T(8,128)S(1)}, f32[24,1,8,16,4]{0,3,4,2,1:T(8,128)S(1)}, u32[]{:S(2)}, u32[]{:S(2)}) collective-permute-start(f32[24,1,8,16,4]{0,3,4,2,1:T(8,128)S(1)} %copy.117), channel_id=1, source_target_pairs={{0,2},{2,4},{4,6},{6,8},{8,10},{10,12},{12,14},{14,16},{16,18},{18... | collective-permute-start | bytes 147464 | tf_op jit(solution)/shard_map/ppermute | solution.py:18
  22.0 2.0 copy.82
  24.1 2.0 copy.84
  27.6 9.4 %broadcast_multiply_fusion = (f32[24,1,8,16,128]{4,0,3,2,1:T(8,128)S(1)}, f32[24,1,8,16,128]{4,0,3,2,1:T(8,128)}) fusion(f32[24,1,8,16,128]{4,0,3,2,1:T(8,128)S(1)} %copy.74, f32[8,16,128]{2,1,0:T(8,128)S(1)} %bitcast.49, f32[24,1,8,16,4]{4,0,3,2,1:T(8,128)} %copy.84, f32[24,1,8,16,4]{4,0,3,2,1:T(8,128)S(1)} %copy-done.6, ...), kind=kLoop, calls=%fused_computation.362 | loop fusion | flops 23199744 | bytes 5668864 | tf_op jit(solution)/shard_map/div | solution.py:84
  37.0 1.7 fusion.246
  38.6 2.3 copy.88
  40.9 1.3 collective-permute-start.6
  43.2 1.6 copy.90
  44.8 5.5 %collective-permute-start.7 = (f32[24,1,8,16,4]{0,3,4,2,1:T(8,128)}, f32[24,1,8,16,4]{0,3,4,2,1:T(8,128)S(1)}, u32[]{:S(2)}, u32[]{:S(2)}) collective-permute-start(f32[24,1,8,16,4]{0,3,4,2,1:T(8,128)} %copy.90), channel_id=1, source_target_pairs={{0,2},{2,4},{4,6},{6,8},{8,10},{10,12},{12,14},{14,16},{16,18},{18... | collective-permute-start | bytes 147464 | tf_op jit(solution)/shard_map/ppermute | solution.py:18
  51.6 6.7 %collective-permute-start.5 = (f32[24,1,8,4,128]{4,0,3,2,1:T(8,128)}, f32[24,1,8,4,128]{4,0,3,2,1:T(8,128)S(1)}, u32[]{:S(2)}, u32[]{:S(2)}) collective-permute-start(f32[24,1,8,4,128]{4,0,3,2,1:T(8,128)} %get-tuple-element.25), channel_id=1, source_target_pairs={{0,8},{2,10},{4,12},{6,14},{8,16},{10,18},{12,20},{14,22},{16,24},... | collective-permute-start | bytes 1179656 | tf_op jit(solution)/shard_map/ppermute | solution.py:18
  59.3 2.0 copy.89
  61.3 2.0 copy.91
  63.2 3.0 %collective-permute-done.4 = f32[24,1,8,4,128]{4,0,3,2,1:T(8,128)S(1)} collective-permute-done((f32[24,1,8,4,128]{4,0,3,2,1:T(8,128)}, f32[24,1,8,4,128]{4,0,3,2,1:T(8,128)S(1)}, u32[]{:S(2)}, u32[]{:S(2)}) %collective-permute-start.4) | collective-permute-done | bytes 393248 | tf_op jit(solution)/shard_map/ppermute | solution.py:18
  66.3 1.3 collective-permute-done.5
  67.6 10.5 %fusion.66 = f32[24,1,8,16,128]{4,0,3,2,1:T(8,128)S(1)} fusion(f32[24,1,8,16,128]{4,0,3,2,1:T(8,128)S(1)} %get-tuple-element.10, f32[24,1,8,4,128]{4,0,3,2,1:T(8,128)S(1)} %broadcast_select_fusion.6, f32[24,1,8,4,128]{4,0,3,2,1:T(8,128)S(1)} %broadcast_select_fusion.7, f32[24,1,8,16,4]{4,0,3,2,1:T(8,128)} %copy.91, f32[24,1,8,16,4]{4,0,3,2,1:T(8,128)} %copy.89, ...), kind=kLoop, calls=%fused_computation.195 | loop fusion | flops 23592960 | bytes 7241728 | tf_op jit(solution)/shard_map/sub | solution.py:87
  78.1 1.7 fusion.244
  79.8 2.3 copy.93
  82.1 1.3 collective-permute-start.10
  84.3 1.6 copy.95
  85.9 3.0 %collective-permute-start.11 = (f32[24,1,8,16,4]{0,3,4,2,1:T(8,128)}, f32[24,1,8,16,4]{0,3,4,2,1:T(8,128)S(1)}, u32[]{:S(2)}, u32[]{:S(2)}) collective-permute-start(f32[24,1,8,16,4]{0,3,4,2,1:T(8,128)} %copy.95), channel_id=1, source_target_pairs={{0,2},{2,4},{4,6},{6,8},{8,10},{10,12},{12,14},{14,16},{16,18},{18... | collective-permute-start | bytes 147464 | tf_op jit(solution)/shard_map/ppermute | solution.py:18
  90.3 4.9 %collective-permute-start.9 = (f32[24,1,8,4,128]{4,0,3,2,1:T(8,128)}, f32[24,1,8,4,128]{4,0,3,2,1:T(8,128)S(1)}, u32[]{:S(2)}, u32[]{:S(2)}) collective-permute-start(f32[24,1,8,4,128]{4,0,3,2,1:T(8,128)} %get-tuple-element.21), channel_id=1, source_target_pairs={{0,8},{2,10},{4,12},{6,14},{8,16},{10,18},{12,20},{14,22},{16,24},... | collective-permute-start | bytes 1179656 | tf_op jit(solution)/shard_map/ppermute | solution.py:18
  96.2 2.0 copy.94
  98.2 2.0 copy.96
  100.2 2.9 %collective-permute-done.8 = f32[24,1,8,4,128]{4,0,3,2,1:T(8,128)S(1)} collective-permute-done((f32[24,1,8,4,128]{4,0,3,2,1:T(8,128)}, f32[24,1,8,4,128]{4,0,3,2,1:T(8,128)S(1)}, u32[]{:S(2)}, u32[]{:S(2)}) %collective-permute-start.8) | collective-permute-done | bytes 393248 | tf_op jit(solution)/shard_map/ppermute | solution.py:18
  103.0 1.8 collective-permute-done.9
  104.9 10.0 %fusion.41 = f32[24,1,8,16,128]{4,0,3,2,1:T(8,128)S(1)} fusion(f32[24,1,8,16,128]{4,0,3,2,1:T(8,128)S(1)} %fusion.66, f32[24,1,8,4,128]{4,0,3,2,1:T(8,128)S(1)} %broadcast_select_fusion.4, f32[24,1,8,4,128]{4,0,3,2,1:T(8,128)S(1)} %broadcast_select_fusion.5, f32[24,1,8,16,4]{4,0,3,2,1:T(8,128)} %copy.96, f32[24,1,8,16,4]{4,0,3,2,1:T(8,128)} %copy.94, ...), kind=kLoop, calls=%fused_computation.170 | loop fusion | flops 23986176 | bytes 5668864 | tf_op jit(solution)/shard_map/sub | solution.py:87
  114.9 2.2 fusion.242
  117.1 2.3 copy.99
  119.4 2.9 %collective-permute-start.15 = (f32[24,1,8,16,4]{0,3,4,2,1:T(8,128)S(1)}, f32[24,1,8,16,4]{0,3,4,2,1:T(8,128)}, u32[]{:S(2)}, u32[]{:S(2)}) collective-permute-start(f32[24,1,8,16,4]{0,3,4,2,1:T(8,128)S(1)} %copy.99), channel_id=1, source_target_pairs={{0,2},{2,4},{4,6},{6,8},{8,10},{10,12},{12,14},{14,16},{16,18},{18... | collective-permute-start | bytes 147464 | tf_op jit(solution)/shard_map/ppermute | solution.py:18
  123.2 3.0 %copy.97 = f32[24,1,8,16,4]{0,3,4,2,1:T(8,128)} copy(f32[24,1,8,16,4]{4,0,3,2,1:T(8,128)} %get-tuple-element.14) | data formatting | bytes 98304 | tf_op jit(solution)/shard_map/slice | solution.py:28
  128.8 8.0 %collective-permute-start.13 = (f32[24,1,8,4,128]{4,0,3,2,1:T(8,128)}, f32[24,1,8,4,128]{4,0,3,2,1:T(8,128)}, u32[]{:S(2)}, u32[]{:S(2)}) collective-permute-start(f32[24,1,8,4,128]{4,0,3,2,1:T(8,128)} %get-tuple-element.17), channel_id=1, source_target_pairs={{0,8},{2,10},{4,12},{6,14},{8,16},{10,18},{12,20},{14,22},{16,24},... | collective-permute-start | bytes 1179656 | tf_op jit(solution)/shard_map/ppermute | solution.py:18
  136.8 2.0 copy.100
  139.8 2.0 copy.98
  141.8 2.9 %collective-permute-done.12 = f32[24,1,8,4,128]{4,0,3,2,1:T(8,128)} collective-permute-done((f32[24,1,8,4,128]{4,0,3,2,1:T(8,128)}, f32[24,1,8,4,128]{4,0,3,2,1:T(8,128)}, u32[]{:S(2)}, u32[]{:S(2)}) %collective-permute-start.12) | collective-permute-done | bytes 393248 | tf_op jit(solution)/shard_map/ppermute | solution.py:18
  145.8 9.5 %fusion.16 = f32[24,1,8,16,128]{4,0,3,2,1:T(8,128)} fusion(f32[24,1,8,16,128]{4,0,3,2,1:T(8,128)S(1)} %fusion.66, f32[24,1,8,16,128]{4,0,3,2,1:T(8,128)S(1)} %fusion.41, f32[24,1,8,4,128]{4,0,3,2,1:T(8,128)S(1)} %broadcast_select_fusion.2, f32[24,1,8,4,128]{4,0,3,2,1:T(8,128)S(1)} %broadcast_select_fusion.3, f32[24,1,8,16,4]{4,0,3,2,1:T(8,128)S(1)} %copy-done.5, ...), kind=kLoop, calls=%fused_computation.145 | loop fusion | flops 23986176 | bytes 5668864 | tf_op jit(solution)/shard_map/mul | solution.py:91
  155.3 1.5 collective-permute-start.16
  156.8 31.7 %collective-permute-done.16 = f32[24,1,8,16,128]{4,0,3,2,1:T(8,128)S(1)} collective-permute-done((f32[24,1,8,16,128]{4,0,3,2,1:T(8,128)}, f32[24,1,8,16,128]{4,0,3,2,1:T(8,128)S(1)}, u32[]{:S(2)}, u32[]{:S(2)}) %collective-permute-start.16) | collective-permute-done | bytes 1572896 | tf_op jit(solution)/shard_map/ppermute | solution.py:94
  188.5 1.7 broadcast_select_fusion.1
  190.2 2.6 %fusion.213 = f32[48,48]{0,1:T(8,128)S(1)} fusion(f32[24,1,8,16,128]{4,0,3,2,1:T(8,128)S(1)} %get-tuple-element.13, f32[24,1,8,16,128]{4,0,3,2,1:T(8,128)S(1)} %get-tuple-element.12), kind=kOutput, calls=%fused_computation.359 | convolution fusion | flops 453771264 | bytes 3154944 | tf_op jit(solution)/shard_map/dot_general | solution.py:57
  194.1 2.7 %collective-permute-start.18 = (f32[48,48]{0,1:T(8,128)S(1)}, f32[48,48]{0,1:T(8,128)S(1)}, u32[]{:S(2)}, u32[]{:S(2)}) collective-permute-start(f32[48,48]{0,1:T(8,128)S(1)} %add.454), channel_id=1, source_target_pairs={{0,4},{2,6},{4,0},{6,2},{8,12},{10,14},{12,8},{14,10},{16,20},{18,... | collective-permute-start | bytes 27656 | tf_op jit(solution)/shard_map/ppermute | solution.py:110
  196.7 1.8 collective-permute-done.18
  198.5 3.2 %collective-permute-start.19 = (f32[48,48]{0,1:T(8,128)S(1)}, f32[48,48]{0,1:T(8,128)S(1)}, u32[]{:S(2)}, u32[]{:S(2)}) collective-permute-start(f32[48,48]{0,1:T(8,128)S(1)} %add.455), channel_id=1, source_target_pairs={{0,8},{2,10},{4,12},{6,14},{8,0},{10,2},{12,4},{14,6},{16,24},{18,... | collective-permute-start | bytes 27656 | tf_op jit(solution)/shard_map/ppermute | solution.py:110
  201.7 1.8 collective-permute-done.19
  203.5 4.1 %collective-permute-start.20 = (f32[48,48]{0,1:T(8,128)S(1)}, f32[48,48]{0,1:T(8,128)S(1)}, u32[]{:S(2)}, u32[]{:S(2)}) collective-permute-start(f32[48,48]{0,1:T(8,128)S(1)} %add.456), channel_id=1, source_target_pairs={{0,16},{2,18},{4,20},{6,22},{8,24},{10,26},{12,28},{14,30},{16,0},... | collective-permute-start | bytes 27656 | tf_op jit(solution)/shard_map/ppermute | solution.py:110
  207.6 1.8 collective-permute-done.20
  209.5 4.4 %cholesky.44 = f32[48,48]{1,0:T(8,128)S(1)} custom-call(f32[48,48]{1,0:T(8,128)S(1)} %fusion.220), custom_call_target="Cholesky" | custom-call | tf_op jit(solution)/shard_map/jit(cholesky)/cholesky | solution.py:62
  215.2 3.7 %custom-call.6 = f32[1,48,48]{1,2,0:T(8,128)S(1)} custom-call(f32[1,48,48]{2,1,0:T(8,128)S(1)} %fusion.224), custom_call_target="InvertDiagBlocksLowerTriangular" | custom-call | tf_op jit(solution)/shard_map/jit(_solve_triangular)/triangular_solve | solution.py:63
  219.1 4.5 %fusion = f32[48,8,16,128]{3,0,2,1:T(8,128)S(1)} fusion(f32[48,48,1,1]{1,0,3,2:T(8,128)S(1)} %convolution_bitcast_fusion.2, f32[24,1,8,16,128]{4,0,3,2,1:T(8,128)} %copy-done.3, f32[24,1,8,16,128]{4,0,3,2,1:T(8,128)} %copy-done.2), kind=kOutput, calls=%fused_computation.105 | convolution fusion | flops 453771264 | bytes 6300672 | tf_op jit(solution)/shard_map/dot_general | solution.py:66
  223.7 2.6 %convolution_bitcast_fusion.1 = f32[48,48]{0,1:T(8,128)S(1)} fusion(f32[48,8,16,128]{3,0,2,1:T(8,128)S(1)} %fusion), kind=kOutput, calls=%fused_computation.360 | convolution fusion | flops 452984832 | bytes 3154944 | tf_op jit(solution)/shard_map/dot_general | solution.py:57
  227.5 2.0 collective-permute-start.22
  229.5 1.8 collective-permute-done.22
  231.4 2.0 collective-permute-start.23
  233.4 1.8 collective-permute-done.23
  235.2 2.9 %collective-permute-start.24 = (f32[48,48]{0,1:T(8,128)S(1)}, f32[48,48]{0,1:T(8,128)S(1)}, u32[]{:S(2)}, u32[]{:S(2)}) collective-permute-start(f32[48,48]{0,1:T(8,128)S(1)} %add.460), channel_id=1, source_target_pairs={{0,16},{2,18},{4,20},{6,22},{8,24},{10,26},{12,28},{14,30},{16,0},... | collective-permute-start | bytes 27656 | tf_op jit(solution)/shard_map/ppermute | solution.py:110
  238.1 1.8 collective-permute-done.24
  240.0 4.4 %cholesky.55 = f32[48,48]{1,0:T(8,128)S(1)} custom-call(f32[48,48]{1,0:T(8,128)S(1)} %fusion.218), custom_call_target="Cholesky" | custom-call | tf_op jit(solution)/shard_map/jit(cholesky)/cholesky | solution.py:62
  245.1 2.1 fusion.227
  247.8 3.7 %custom-call.7 = f32[1,48,48]{1,2,0:T(8,128)S(1)} custom-call(f32[1,48,48]{2,1,0:T(8,128)S(1)} %select_bitcast_fusion), custom_call_target="InvertDiagBlocksLowerTriangular" | custom-call | tf_op jit(solution)/shard_map/jit(_solve_triangular)/triangular_solve | solution.py:63
  251.7 1.6 convolution_bitcast_fusion
  253.4 1.4 copy.107
  (79 shorter events, 25.1 us)
Async XLA Ops:
  3.0 8.0 %copy-start = (f32[24,1,8,16,128]{4,3,2,1,0:T(8,128)S(1)}, f32[24,1,8,16,128]{4,3,2,1,0:T(8,128)}, u32[]{:S(2)}) copy-start(f32[24,1,8,16,128]{4,3,2,1,0:T(8,128)} %param.5) | copy-start | bytes 4718596
  3.9 22.1 %collective-permute-start.1 = (f32[24,1,8,4,128]{4,0,3,2,1:T(8,128)}, f32[24,1,8,4,128]{4,0,3,2,1:T(8,128)}, u32[]{:S(2)}, u32[]{:S(2)}) collective-permute-start(f32[24,1,8,4,128]{4,0,3,2,1:T(8,128)} %get-tuple-element.27), channel_id=1, source_target_pairs={{0,8},{2,10},{4,12},{6,14},{8,16},{10,18},{12,20},{14,22},{16,24},... | collective-permute-start | bytes 1179656 | tf_op jit(solution)/shard_map/ppermute | solution.py:18
  9.6 16.5 %collective-permute-start = (f32[24,1,8,4,128]{4,0,3,2,1:T(8,128)}, f32[24,1,8,4,128]{4,0,3,2,1:T(8,128)}, u32[]{:S(2)}, u32[]{:S(2)}) collective-permute-start(f32[24,1,8,4,128]{4,0,3,2,1:T(8,128)} %get-tuple-element.26), channel_id=1, source_target_pairs={{8,0},{10,2},{12,4},{14,6},{16,8},{18,10},{20,12},{22,14},{24,16},... | collective-permute-start | bytes 1179656 | tf_op jit(solution)/shard_map/ppermute | solution.py:18
  12.6 8.3 %copy-start.7 = (f32[1,8,16,128]{3,2,1,0:T(8,128)S(1)}, f32[1,8,16,128]{3,2,1,0:T(8,128)}, u32[]{:S(2)}) copy-start(f32[1,8,16,128]{3,2,1,0:T(8,128)} %param.6) | copy-start | bytes 196612
  15.7 5.4 %collective-permute-start.2 = (f32[24,1,8,16,4]{0,3,4,2,1:T(8,128)}, f32[24,1,8,16,4]{0,3,4,2,1:T(8,128)}, u32[]{:S(2)}, u32[]{:S(2)}) collective-permute-start(f32[24,1,8,16,4]{0,3,4,2,1:T(8,128)} %copy.116), channel_id=1, source_target_pairs={{2,0},{4,2},{6,4},{8,6},{10,8},{12,10},{14,12},{16,14},{18,16},{20... | collective-permute-start | bytes 147464 | tf_op jit(solution)/shard_map/ppermute | solution.py:18
  17.9 6.1 %collective-permute-start.3 = (f32[24,1,8,16,4]{0,3,4,2,1:T(8,128)S(1)}, f32[24,1,8,16,4]{0,3,4,2,1:T(8,128)S(1)}, u32[]{:S(2)}, u32[]{:S(2)}) collective-permute-start(f32[24,1,8,16,4]{0,3,4,2,1:T(8,128)S(1)} %copy.117), channel_id=1, source_target_pairs={{0,2},{2,4},{4,6},{6,8},{8,10},{10,12},{12,14},{14,16},{16,18},{18... | collective-permute-start | bytes 147464 | tf_op jit(solution)/shard_map/ppermute | solution.py:18
  26.1 1.5 copy-start.6
  40.9 17.3 %collective-permute-start.6 = (f32[24,1,8,16,4]{0,3,4,2,1:T(8,128)S(1)}, f32[24,1,8,16,4]{0,3,4,2,1:T(8,128)}, u32[]{:S(2)}, u32[]{:S(2)}) collective-permute-start(f32[24,1,8,16,4]{0,3,4,2,1:T(8,128)S(1)} %copy.88), channel_id=1, source_target_pairs={{2,0},{4,2},{6,4},{8,6},{10,8},{12,10},{14,12},{16,14},{18,16},{20... | collective-permute-start | bytes 147464 | tf_op jit(solution)/shard_map/ppermute | solution.py:18
  44.8 16.5 %collective-permute-start.7 = (f32[24,1,8,16,4]{0,3,4,2,1:T(8,128)}, f32[24,1,8,16,4]{0,3,4,2,1:T(8,128)S(1)}, u32[]{:S(2)}, u32[]{:S(2)}) collective-permute-start(f32[24,1,8,16,4]{0,3,4,2,1:T(8,128)} %copy.90), channel_id=1, source_target_pairs={{0,2},{2,4},{4,6},{6,8},{8,10},{10,12},{12,14},{14,16},{16,18},{18... | collective-permute-start | bytes 147464 | tf_op jit(solution)/shard_map/ppermute | solution.py:18
  50.3 16.0 %collective-permute-start.4 = (f32[24,1,8,4,128]{4,0,3,2,1:T(8,128)}, f32[24,1,8,4,128]{4,0,3,2,1:T(8,128)S(1)}, u32[]{:S(2)}, u32[]{:S(2)}) collective-permute-start(f32[24,1,8,4,128]{4,0,3,2,1:T(8,128)} %get-tuple-element.24), channel_id=1, source_target_pairs={{8,0},{10,2},{12,4},{14,6},{16,8},{18,10},{20,12},{22,14},{24,16},... | collective-permute-start | bytes 1179656 | tf_op jit(solution)/shard_map/ppermute | solution.py:18
  51.6 16.0 %collective-permute-start.5 = (f32[24,1,8,4,128]{4,0,3,2,1:T(8,128)}, f32[24,1,8,4,128]{4,0,3,2,1:T(8,128)S(1)}, u32[]{:S(2)}, u32[]{:S(2)}) collective-permute-start(f32[24,1,8,4,128]{4,0,3,2,1:T(8,128)} %get-tuple-element.25), channel_id=1, source_target_pairs={{0,8},{2,10},{4,12},{6,14},{8,16},{10,18},{12,20},{14,22},{16,24},... | collective-permute-start | bytes 1179656 | tf_op jit(solution)/shard_map/ppermute | solution.py:18
  63.2 4.4 %copy-start.1 = (f32[24,1,8,16,128]{4,3,2,1,0:T(8,128)S(1)}, f32[24,1,8,16,128]{4,3,2,1,0:T(8,128)}, u32[]{:S(2)}) copy-start(f32[24,1,8,16,128]{4,3,2,1,0:T(8,128)} %param.5) | copy-start | bytes 4718596
  82.1 13.1 %collective-permute-start.10 = (f32[24,1,8,16,4]{0,3,4,2,1:T(8,128)S(1)}, f32[24,1,8,16,4]{0,3,4,2,1:T(8,128)}, u32[]{:S(2)}, u32[]{:S(2)}) collective-permute-start(f32[24,1,8,16,4]{0,3,4,2,1:T(8,128)S(1)} %copy.93), channel_id=1, source_target_pairs={{2,0},{4,2},{6,4},{8,6},{10,8},{12,10},{14,12},{16,14},{18,16},{20... | collective-permute-start | bytes 147464 | tf_op jit(solution)/shard_map/ppermute | solution.py:18
  85.9 12.2 %collective-permute-start.11 = (f32[24,1,8,16,4]{0,3,4,2,1:T(8,128)}, f32[24,1,8,16,4]{0,3,4,2,1:T(8,128)S(1)}, u32[]{:S(2)}, u32[]{:S(2)}) collective-permute-start(f32[24,1,8,16,4]{0,3,4,2,1:T(8,128)} %copy.95), channel_id=1, source_target_pairs={{0,2},{2,4},{4,6},{6,8},{8,10},{10,12},{12,14},{14,16},{16,18},{18... | collective-permute-start | bytes 147464 | tf_op jit(solution)/shard_map/ppermute | solution.py:18
  89.0 14.0 %collective-permute-start.8 = (f32[24,1,8,4,128]{4,0,3,2,1:T(8,128)}, f32[24,1,8,4,128]{4,0,3,2,1:T(8,128)S(1)}, u32[]{:S(2)}, u32[]{:S(2)}) collective-permute-start(f32[24,1,8,4,128]{4,0,3,2,1:T(8,128)} %get-tuple-element.20), channel_id=1, source_target_pairs={{8,0},{10,2},{12,4},{14,6},{16,8},{18,10},{20,12},{22,14},{24,16},... | collective-permute-start | bytes 1179656 | tf_op jit(solution)/shard_map/ppermute | solution.py:18
  90.3 14.6 %collective-permute-start.9 = (f32[24,1,8,4,128]{4,0,3,2,1:T(8,128)}, f32[24,1,8,4,128]{4,0,3,2,1:T(8,128)S(1)}, u32[]{:S(2)}, u32[]{:S(2)}) collective-permute-start(f32[24,1,8,4,128]{4,0,3,2,1:T(8,128)} %get-tuple-element.21), channel_id=1, source_target_pairs={{0,8},{2,10},{4,12},{6,14},{8,16},{10,18},{12,20},{14,22},{16,24},... | collective-permute-start | bytes 1179656 | tf_op jit(solution)/shard_map/ppermute | solution.py:18
  100.1 4.7 %copy-start.4 = (f32[24,1,8,16,128]{4,0,3,2,1:T(8,128)S(1)}, f32[24,1,8,16,128]{4,0,3,2,1:T(8,128)}, u32[]{:S(2)}) copy-start(f32[24,1,8,16,128]{4,0,3,2,1:T(8,128)} %get-tuple-element.11) | copy-start | bytes 4718596
  119.4 17.4 %collective-permute-start.15 = (f32[24,1,8,16,4]{0,3,4,2,1:T(8,128)S(1)}, f32[24,1,8,16,4]{0,3,4,2,1:T(8,128)}, u32[]{:S(2)}, u32[]{:S(2)}) collective-permute-start(f32[24,1,8,16,4]{0,3,4,2,1:T(8,128)S(1)} %copy.99), channel_id=1, source_target_pairs={{0,2},{2,4},{4,6},{6,8},{8,10},{10,12},{12,14},{14,16},{16,18},{18... | collective-permute-start | bytes 147464 | tf_op jit(solution)/shard_map/ppermute | solution.py:18
  126.2 12.6 %collective-permute-start.14 = (f32[24,1,8,16,4]{0,3,4,2,1:T(8,128)}, f32[24,1,8,16,4]{0,3,4,2,1:T(8,128)}, u32[]{:S(2)}, u32[]{:S(2)}) collective-permute-start(f32[24,1,8,16,4]{0,3,4,2,1:T(8,128)} %copy.97), channel_id=1, source_target_pairs={{2,0},{4,2},{6,4},{8,6},{10,8},{12,10},{14,12},{16,14},{18,16},{20... | collective-permute-start | bytes 147464 | tf_op jit(solution)/shard_map/ppermute | solution.py:18
  127.5 17.2 %collective-permute-start.12 = (f32[24,1,8,4,128]{4,0,3,2,1:T(8,128)}, f32[24,1,8,4,128]{4,0,3,2,1:T(8,128)}, u32[]{:S(2)}, u32[]{:S(2)}) collective-permute-start(f32[24,1,8,4,128]{4,0,3,2,1:T(8,128)} %get-tuple-element.16), channel_id=1, source_target_pairs={{8,0},{10,2},{12,4},{14,6},{16,8},{18,10},{20,12},{22,14},{24,16},... | collective-permute-start | bytes 1179656 | tf_op jit(solution)/shard_map/ppermute | solution.py:18
  128.8 16.9 %collective-permute-start.13 = (f32[24,1,8,4,128]{4,0,3,2,1:T(8,128)}, f32[24,1,8,4,128]{4,0,3,2,1:T(8,128)}, u32[]{:S(2)}, u32[]{:S(2)}) collective-permute-start(f32[24,1,8,4,128]{4,0,3,2,1:T(8,128)} %get-tuple-element.17), channel_id=1, source_target_pairs={{0,8},{2,10},{4,12},{6,14},{8,16},{10,18},{12,20},{14,22},{16,24},... | collective-permute-start | bytes 1179656 | tf_op jit(solution)/shard_map/ppermute | solution.py:18
  141.8 4.0 %copy-start.5 = (f32[24,1,8,16,4]{4,0,3,2,1:T(8,128)S(1)}, f32[24,1,8,16,4]{4,0,3,2,1:T(8,128)}, u32[]{:S(2)}) copy-start(f32[24,1,8,16,4]{4,0,3,2,1:T(8,128)} %copy.100) | copy-start | bytes 147460
  155.3 33.2 %collective-permute-start.16 = (f32[24,1,8,16,128]{4,0,3,2,1:T(8,128)}, f32[24,1,8,16,128]{4,0,3,2,1:T(8,128)S(1)}, u32[]{:S(2)}, u32[]{:S(2)}) collective-permute-start(f32[24,1,8,16,128]{4,0,3,2,1:T(8,128)} %fusion.16), channel_id=1, source_target_pairs={{0,1},{1,0},{2,3},{3,2},{4,5},{5,4},{6,7},{7,6},{8,9},{9,8},{10,11... | collective-permute-start | bytes 4718600 | tf_op jit(solution)/shard_map/ppermute | solution.py:94
  190.2 2.6 %copy-start.2 = (f32[24,1,8,16,128]{4,0,3,2,1:T(8,128)}, f32[24,1,8,16,128]{4,0,3,2,1:T(8,128)S(1)}, u32[]{:S(2)}) copy-start(f32[24,1,8,16,128]{4,0,3,2,1:T(8,128)S(1)} %get-tuple-element.12) | copy-start | bytes 4718596
  190.2 2.6 %copy-start.3 = (f32[24,1,8,16,128]{4,0,3,2,1:T(8,128)}, f32[24,1,8,16,128]{4,0,3,2,1:T(8,128)S(1)}, u32[]{:S(2)}) copy-start(f32[24,1,8,16,128]{4,0,3,2,1:T(8,128)S(1)} %get-tuple-element.13) | copy-start | bytes 4718596
  192.8 1.3 collective-permute-start.17
  194.1 4.5 %collective-permute-start.18 = (f32[48,48]{0,1:T(8,128)S(1)}, f32[48,48]{0,1:T(8,128)S(1)}, u32[]{:S(2)}, u32[]{:S(2)}) collective-permute-start(f32[48,48]{0,1:T(8,128)S(1)} %add.454), channel_id=1, source_target_pairs={{0,4},{2,6},{4,0},{6,2},{8,12},{10,14},{12,8},{14,10},{16,20},{18,... | collective-permute-start | bytes 27656 | tf_op jit(solution)/shard_map/ppermute | solution.py:110
  198.5 5.0 %collective-permute-start.19 = (f32[48,48]{0,1:T(8,128)S(1)}, f32[48,48]{0,1:T(8,128)S(1)}, u32[]{:S(2)}, u32[]{:S(2)}) collective-permute-start(f32[48,48]{0,1:T(8,128)S(1)} %add.455), channel_id=1, source_target_pairs={{0,8},{2,10},{4,12},{6,14},{8,0},{10,2},{12,4},{14,6},{16,24},{18,... | collective-permute-start | bytes 27656 | tf_op jit(solution)/shard_map/ppermute | solution.py:110
  203.5 5.9 %collective-permute-start.20 = (f32[48,48]{0,1:T(8,128)S(1)}, f32[48,48]{0,1:T(8,128)S(1)}, u32[]{:S(2)}, u32[]{:S(2)}) collective-permute-start(f32[48,48]{0,1:T(8,128)S(1)} %add.456), channel_id=1, source_target_pairs={{0,16},{2,18},{4,20},{6,22},{8,24},{10,26},{12,28},{14,30},{16,0},... | collective-permute-start | bytes 27656 | tf_op jit(solution)/shard_map/ppermute | solution.py:110
  226.2 1.3 collective-permute-start.21
  227.5 3.8 %collective-permute-start.22 = (f32[48,48]{0,1:T(8,128)S(1)}, f32[48,48]{0,1:T(8,128)S(1)}, u32[]{:S(2)}, u32[]{:S(2)}) collective-permute-start(f32[48,48]{0,1:T(8,128)S(1)} %add.458), channel_id=1, source_target_pairs={{0,4},{2,6},{4,0},{6,2},{8,12},{10,14},{12,8},{14,10},{16,20},{18,... | collective-permute-start | bytes 27656 | tf_op jit(solution)/shard_map/ppermute | solution.py:110
  231.4 3.8 %collective-permute-start.23 = (f32[48,48]{0,1:T(8,128)S(1)}, f32[48,48]{0,1:T(8,128)S(1)}, u32[]{:S(2)}, u32[]{:S(2)}) collective-permute-start(f32[48,48]{0,1:T(8,128)S(1)} %add.459), channel_id=1, source_target_pairs={{0,8},{2,10},{4,12},{6,14},{8,0},{10,2},{12,4},{14,6},{16,24},{18,... | collective-permute-start | bytes 27656 | tf_op jit(solution)/shard_map/ppermute | solution.py:110
  235.2 4.7 %collective-permute-start.24 = (f32[48,48]{0,1:T(8,128)S(1)}, f32[48,48]{0,1:T(8,128)S(1)}, u32[]{:S(2)}, u32[]{:S(2)}) collective-permute-start(f32[48,48]{0,1:T(8,128)S(1)} %add.460), channel_id=1, source_target_pairs={{0,16},{2,18},{4,20},{6,22},{8,24},{10,26},{12,28},{14,30},{16,0},... | collective-permute-start | bytes 27656 | tf_op jit(solution)/shard_map/ppermute | solution.py:110

commit v3 on v2

--- a/solution.py
+++ b/solution.py
@@ -27,12 +27,15 @@
     top_layers = lax.slice_in_dim(field_in, extent - 4, extent, axis=axis_dim)
     bottom_layers = lax.slice_in_dim(field_in, 0, 4, axis=axis_dim)
     received = []
-    for direction, portion, retain in (
-        (1, top_layers, coordinate > 0),
-        (-1, bottom_layers, coordinate < tile_count - 1),
-    ):
-        arrived = shifted(portion, "space", direction * stride)
-        received.append(jnp.where(retain, arrived, jnp.zeros_like(arrived)))
+    devices = range(lax.axis_size("space"))
+    for direction, portion in ((1, top_layers), (-1, bottom_layers)):
+        distance = direction * stride
+        route = [
+            (i - distance, i)
+            for i in devices
+            if i - distance in devices and 0 <= (i // stride) % tile_count - direction < tile_count
+        ]
+        received.append(lax.ppermute(portion, "space", route))
     return jnp.concatenate([received[0], field_in, received[1]], axis=axis_dim)
 
 

time: 256 us -> 264 us (1.031)
  local copies, waits for them, and re-layouts: 48.3 us -> 58.3 us
  starting transfers between devices: 68.6 us -> 60.8 us
  other arithmetic: 66.1 us -> 72.2 us
    ppermute x0 -> x8, local copies, waits for them, and re-layouts: none -> 21.6 us  [padded_along(): received.append(lax.ppermute(portion, 'space', route))]
    select_n x8 -> x0, local copies, waits for them, and re-layouts: 15.8 us -> none  [padded_along(): received.append(jnp.where(retain, arrived, jnp.zeros_like(arrived)))]
    sub x2, other arithmetic: 20.4 us -> 33.5 us  [shards(): 2.0 * (hamiltonian(current, potential, layout) - centre_value * current)]
    ppermute x16, waiting for transfers between devices: 11.9 us -> 5.56 us  [padded_along(): received.append(lax.ppermute(portion, 'space', route))]
    select_n x16 -> x0, other arithmetic: 6.34 us -> none  [padded_along(): received.append(jnp.where(retain, arrived, jnp.zeros_like(arrived)))]
    ppermute x8, starting transfers between devices: 17 us -> 12.1 us  [reduce_everywhere(): total = total + lax.ppermute(total, 'space', route)]
    ppermute x8, waiting for transfers between devices: 13.2 us -> 17.1 us  [reduce_everywhere(): total = total + lax.ppermute(total, 'space', route)]
    ppermute x16, starting transfers between devices: 50.1 us -> 47.1 us  [padded_along(): received.append(lax.ppermute(portion, 'space', route))]
  transfers between devices with their start and end apart: 25 -> 25, of which waited for: 14 -> 10; matrix products, arithmetic and copies ran while one was open for 14% -> 19% of each run, Pallas kernels for 0% -> 0%
where the time goes in v3:
time: 264 us; the launch traced here: 263 us
  other arithmetic  72.2 us (27%)
  starting transfers between devices  60.8 us (23%)
  local copies, waits for them, and re-layouts  58.3 us (22%)
  waiting for transfers between devices  56.7 us (21%)
  matrix products  13.9 us (5%)
    ppermute x16, starting transfers between devices, padded_along(): received.append(lax.ppermute(portion, 'space', route))  47.1 us
    ppermute x1, waiting for transfers between devices, shards(): other = lax.ppermute(filtered, 'band', [(0, 1), (1, 0)])  34.1 us
    sub x2, other arithmetic, shards(): 2.0 * (hamiltonian(current, potential, layout) - centre_value * current)  33.5 us
    ppermute x8, local copies, waits for them, and re-layouts, padded_along(): received.append(lax.ppermute(portion, 'space', route))  21.6 us
    slice x11, local copies, waits for them, and re-layouts, padded_along(): bottom_layers = lax.slice_in_dim(field_in, 0, 4, axis=axis_dim)  18.6 us
    ppermute x8, waiting for transfers between devices, reduce_everywhere(): total = total + lax.ppermute(total, 'space', route)  17.1 us
    ppermute x8, starting transfers between devices, reduce_everywhere(): total = total + lax.ppermute(total, 'space', route)  12.1 us
    mul x1, other arithmetic, shards(): filtered = current * filter_scale  11 us
  transfers between devices with their start and end apart: 25, of which 10 were waited for; matrix products, arithmetic and copies ran while one was open for 19% of the time, Pallas kernels for 0%

profile of v3, /device:TPU:0, one launch (start us, length us, event | category | flops | bytes accessed | tf_op | source)
XLA Modules:
  0.0 262.9 jit_solution(1309759675643525224)
XLA Ops:
  0.6 2.3 copy.24
  3.9 5.0 %collective-permute-start.1 = (f32[24,1,8,4,128]{4,0,3,2,1:T(8,128)}, f32[24,1,8,4,128]{4,0,3,2,1:T(8,128)S(1)}, u32[]{:S(2)}, u32[]{:S(2)}) collective-permute-start(f32[24,1,8,4,128]{4,0,3,2,1:T(8,128)} %get-tuple-element.25), channel_id=1, source_target_pairs={{0,8},{2,10},{4,12},{6,14},{8,16},{10,18},{12,20},{14,22},{16,24},... | collective-permute-start | bytes 1179656 | tf_op jit(solution)/shard_map/ppermute | solution.py:38
  8.9 2.3 fusion.239
  11.2 3.0 %copy.66 = f32[24,1,8,16,4]{0,3,4,2,1:T(8,128)} copy(f32[24,1,8,16,4]{4,3,2,1,0:T(8,128)} %get-tuple-element.28) | data formatting | bytes 98304
  14.2 1.3 collective-permute-start.2
  15.4 3.0 %copy.67 = f32[24,1,8,16,4]{0,3,4,2,1:T(8,128)} copy(f32[24,1,8,16,4]{4,3,2,1,0:T(8,128)} %get-tuple-element.29) | data formatting | bytes 98304
  18.4 3.7 %collective-permute-start.3 = (f32[24,1,8,16,4]{0,3,4,2,1:T(8,128)}, f32[24,1,8,16,4]{0,3,4,2,1:T(8,128)}, u32[]{:S(2)}, u32[]{:S(2)}) collective-permute-start(f32[24,1,8,16,4]{0,3,4,2,1:T(8,128)} %copy.67), channel_id=1, source_target_pairs={{0,2},{2,4},{4,6},{8,10},{10,12},{12,14},{16,18},{18,20},{20,22},{... | collective-permute-start | bytes 147464 | tf_op jit(solution)/shard_map/ppermute | solution.py:38
  22.1 1.3 collective-permute-start
  23.4 3.0 %copy.32 = f32[24,1,8,16,4]{4,0,3,2,1:T(8,128)} copy(f32[24,1,8,16,4]{0,3,4,2,1:T(8,128)} %collective-permute-done.2) | data formatting | bytes 98304 | tf_op jit(solution)/shard_map/ppermute | solution.py:38
  26.4 2.9 %copy.34 = f32[24,1,8,16,4]{4,0,3,2,1:T(8,128)} copy(f32[24,1,8,16,4]{0,3,4,2,1:T(8,128)} %collective-permute-done.3) | data formatting | bytes 98304 | tf_op jit(solution)/shard_map/ppermute | solution.py:38
  30.3 5.5 %collective-permute-done = f32[24,1,8,4,128]{4,0,3,2,1:T(8,128)} collective-permute-done((f32[24,1,8,4,128]{4,0,3,2,1:T(8,128)}, f32[24,1,8,4,128]{4,0,3,2,1:T(8,128)}, u32[]{:S(2)}, u32[]{:S(2)}) %collective-permute-start) | collective-permute-done | bytes 393248 | tf_op jit(solution)/shard_map/ppermute | solution.py:38
  36.9 7.2 %broadcast_multiply_fusion = (f32[24,1,8,16,128]{4,0,3,2,1:T(8,128)S(1)}, f32[24,1,8,16,128]{4,0,3,2,1:T(8,128)}) fusion(f32[24,1,8,16,128]{4,0,3,2,1:T(8,128)S(1)} %copy.24, f32[8,16,128]{2,1,0:T(8,128)S(1)} %bitcast.49, f32[24,1,8,16,4]{4,0,3,2,1:T(8,128)S(1)} %copy-done.5, f32[24,1,8,16,4]{4,0,3,2,1:T(8,128)S(1)} %copy-done.4, ...), kind=kLoop, calls=%fused_computation.342 | loop fusion | flops 20054016 | bytes 17465344 | tf_op jit(solution)/shard_map/div | solution.py:87
  45.1 1.3 collective-permute-start.4
  46.4 5.3 %collective-permute-start.5 = (f32[24,1,8,4,128]{4,0,3,2,1:T(8,128)}, f32[24,1,8,4,128]{4,0,3,2,1:T(8,128)}, u32[]{:S(2)}, u32[]{:S(2)}) collective-permute-start(f32[24,1,8,4,128]{4,0,3,2,1:T(8,128)} %get-tuple-element.23), channel_id=1, source_target_pairs={{0,8},{2,10},{4,12},{6,14},{8,16},{10,18},{12,20},{14,22},{16,24},... | collective-permute-start | bytes 1179656 | tf_op jit(solution)/shard_map/ppermute | solution.py:38
  51.7 1.7 fusion.236
  53.4 2.3 copy.38
  55.7 1.3 collective-permute-start.6
  57.0 1.6 copy.40
  58.6 3.2 %collective-permute-start.7 = (f32[24,1,8,16,4]{0,3,4,2,1:T(8,128)}, f32[24,1,8,16,4]{0,3,4,2,1:T(8,128)S(1)}, u32[]{:S(2)}, u32[]{:S(2)}) collective-permute-start(f32[24,1,8,16,4]{0,3,4,2,1:T(8,128)} %copy.40), channel_id=1, source_target_pairs={{0,2},{2,4},{4,6},{8,10},{10,12},{12,14},{16,18},{18,20},{20,22},{... | collective-permute-start | bytes 147464 | tf_op jit(solution)/shard_map/ppermute | solution.py:38
  61.8 2.9 %copy.39 = f32[24,1,8,16,4]{4,0,3,2,1:T(8,128)} copy(f32[24,1,8,16,4]{0,3,4,2,1:T(8,128)} %collective-permute-done.6) | data formatting | bytes 98304 | tf_op jit(solution)/shard_map/ppermute | solution.py:38
  64.7 2.0 copy.41
  66.7 22.9 %fusion.66 = f32[24,1,8,16,128]{4,0,3,2,1:T(8,128)S(1)} fusion(f32[24,1,8,16,128]{4,0,3,2,1:T(8,128)} %copy-done.1, f32[24,1,8,4,128]{4,0,3,2,1:T(8,128)} %collective-permute-done.5, f32[24,1,8,4,128]{4,0,3,2,1:T(8,128)} %collective-permute-done.4, f32[24,1,8,16,4]{4,0,3,2,1:T(8,128)} %copy.41, f32[24,1,8,16,4]{4,0,3,2,1:T(8,128)} %copy.39, ...), kind=kLoop, calls=%fused_computation.183 | loop fusion | flops 23592960 | bytes 7241728 | tf_op jit(solution)/shard_map/sub | solution.py:90
  91.9 5.3 %collective-permute-start.9 = (f32[24,1,8,4,128]{4,0,3,2,1:T(8,128)}, f32[24,1,8,4,128]{4,0,3,2,1:T(8,128)}, u32[]{:S(2)}, u32[]{:S(2)}) collective-permute-start(f32[24,1,8,4,128]{4,0,3,2,1:T(8,128)} %get-tuple-element.19), channel_id=1, source_target_pairs={{0,8},{2,10},{4,12},{6,14},{8,16},{10,18},{12,20},{14,22},{16,24},... | collective-permute-start | bytes 1179656 | tf_op jit(solution)/shard_map/ppermute | solution.py:38
  97.2 1.7 fusion.234
  99.0 2.3 copy.43
  101.3 1.3 collective-permute-start.10
  102.6 1.6 copy.45
  104.2 3.0 %collective-permute-start.11 = (f32[24,1,8,16,4]{0,3,4,2,1:T(8,128)}, f32[24,1,8,16,4]{0,3,4,2,1:T(8,128)S(1)}, u32[]{:S(2)}, u32[]{:S(2)}) collective-permute-start(f32[24,1,8,16,4]{0,3,4,2,1:T(8,128)} %copy.45), channel_id=1, source_target_pairs={{0,2},{2,4},{4,6},{8,10},{10,12},{12,14},{16,18},{18,20},{20,22},{... | collective-permute-start | bytes 147464 | tf_op jit(solution)/shard_map/ppermute | solution.py:38
  107.2 3.0 %copy.44 = f32[24,1,8,16,4]{4,0,3,2,1:T(8,128)} copy(f32[24,1,8,16,4]{0,3,4,2,1:T(8,128)} %collective-permute-done.10) | data formatting | bytes 98304 | tf_op jit(solution)/shard_map/ppermute | solution.py:38
  110.2 2.0 copy.46
  112.2 10.5 %fusion.41 = f32[24,1,8,16,128]{4,0,3,2,1:T(8,128)S(1)} fusion(f32[24,1,8,16,128]{4,0,3,2,1:T(8,128)S(1)} %fusion.66, f32[24,1,8,4,128]{4,0,3,2,1:T(8,128)} %collective-permute-done.9, f32[24,1,8,4,128]{4,0,3,2,1:T(8,128)} %collective-permute-done.8, f32[24,1,8,16,4]{4,0,3,2,1:T(8,128)} %copy.46, f32[24,1,8,16,4]{4,0,3,2,1:T(8,128)} %copy.44, ...), kind=kLoop, calls=%fused_computation.158 | loop fusion | flops 23986176 | bytes 5668864 | tf_op jit(solution)/shard_map/sub | solution.py:90
  125.0 5.3 %collective-permute-start.13 = (f32[24,1,8,4,128]{4,0,3,2,1:T(8,128)}, f32[24,1,8,4,128]{4,0,3,2,1:T(8,128)}, u32[]{:S(2)}, u32[]{:S(2)}) collective-permute-start(f32[24,1,8,4,128]{4,0,3,2,1:T(8,128)} %get-tuple-element.15), channel_id=1, source_target_pairs={{0,8},{2,10},{4,12},{6,14},{8,16},{10,18},{12,20},{14,22},{16,24},... | collective-permute-start | bytes 1179656 | tf_op jit(solution)/shard_map/ppermute | solution.py:38
  130.3 2.2 fusion.232
  132.5 2.3 copy.47
  134.8 1.3 collective-permute-start.14
  136.1 3.0 %copy.49 = f32[24,1,8,16,4]{0,3,4,2,1:T(8,128)} copy(f32[24,1,8,16,4]{4,0,3,2,1:T(8,128)} %get-tuple-element.13) | data formatting | bytes 98304 | tf_op jit(solution)/shard_map/slice | solution.py:27
  139.1 5.9 %collective-permute-start.15 = (f32[24,1,8,16,4]{0,3,4,2,1:T(8,128)}, f32[24,1,8,16,4]{0,3,4,2,1:T(8,128)}, u32[]{:S(2)}, u32[]{:S(2)}) collective-permute-start(f32[24,1,8,16,4]{0,3,4,2,1:T(8,128)} %copy.49), channel_id=1, source_target_pairs={{0,2},{2,4},{4,6},{8,10},{10,12},{12,14},{16,18},{18,20},{20,22},{... | collective-permute-start | bytes 147464 | tf_op jit(solution)/shard_map/ppermute | solution.py:38
  145.1 3.0 %copy.48 = f32[24,1,8,16,4]{4,0,3,2,1:T(8,128)} copy(f32[24,1,8,16,4]{0,3,4,2,1:T(8,128)} %collective-permute-done.14) | data formatting | bytes 98304 | tf_op jit(solution)/shard_map/ppermute | solution.py:38
  148.0 2.9 %copy.50 = f32[24,1,8,16,4]{4,0,3,2,1:T(8,128)} copy(f32[24,1,8,16,4]{0,3,4,2,1:T(8,128)} %collective-permute-done.15) | data formatting | bytes 98304 | tf_op jit(solution)/shard_map/ppermute | solution.py:38
  150.9 11.0 %fusion.16 = f32[24,1,8,16,128]{4,0,3,2,1:T(8,128)} fusion(f32[24,1,8,16,128]{4,0,3,2,1:T(8,128)S(1)} %fusion.66, f32[24,1,8,16,128]{4,0,3,2,1:T(8,128)S(1)} %fusion.41, f32[24,1,8,4,128]{4,0,3,2,1:T(8,128)} %collective-permute-done.13, f32[24,1,8,4,128]{4,0,3,2,1:T(8,128)} %collective-permute-done.12, f32[24,1,8,16,4]{4,0,3,2,1:T(8,128)} %copy.50, ...), kind=kLoop, calls=%fused_computation.133 | loop fusion | flops 23986176 | bytes 5668864 | tf_op jit(solution)/shard_map/mul | solution.py:94
  161.9 1.6 collective-permute-start.16
  163.5 34.1 %collective-permute-done.16 = f32[24,1,8,16,128]{4,0,3,2,1:T(8,128)S(1)} collective-permute-done((f32[24,1,8,16,128]{4,0,3,2,1:T(8,128)}, f32[24,1,8,16,128]{4,0,3,2,1:T(8,128)S(1)}, u32[]{:S(2)}, u32[]{:S(2)}) %collective-permute-start.16) | collective-permute-done | bytes 1572896 | tf_op jit(solution)/shard_map/ppermute | solution.py:97
  197.6 1.7 broadcast_select_fusion.1
  199.3 2.6 fusion.203
  201.9 1.8 collective-permute-start.17
  204.5 2.5 collective-permute-start.18
  207.0 1.8 collective-permute-done.18
  209.2 3.4 %collective-permute-done.19 = f32[48,48]{0,1:T(8,128)S(1)} collective-permute-done((f32[48,48]{0,1:T(8,128)S(1)}, f32[48,48]{0,1:T(8,128)S(1)}, u32[]{:S(2)}, u32[]{:S(2)}) %collective-permute-start.19) | collective-permute-done | bytes 9248 | tf_op jit(solution)/shard_map/ppermute | solution.py:113
  212.7 2.6 collective-permute-start.20
  215.2 2.2 collective-permute-done.20
  217.6 4.4 %cholesky.44 = f32[48,48]{1,0:T(8,128)S(1)} custom-call(f32[48,48]{1,0:T(8,128)S(1)} %fusion.210), custom_call_target="Cholesky" | custom-call | tf_op jit(solution)/shard_map/jit(cholesky)/cholesky | solution.py:65
  223.3 3.7 %custom-call.6 = f32[1,48,48]{1,2,0:T(8,128)S(1)} custom-call(f32[1,48,48]{2,1,0:T(8,128)S(1)} %fusion.214), custom_call_target="InvertDiagBlocksLowerTriangular" | custom-call | tf_op jit(solution)/shard_map/jit(_solve_triangular)/triangular_solve | solution.py:66
  227.2 4.5 %fusion = f32[48,8,16,128]{3,0,2,1:T(8,128)S(1)} fusion(f32[48,48,1,1]{1,0,3,2:T(8,128)S(1)} %convolution_bitcast_fusion.2, f32[24,1,8,16,128]{4,0,3,2,1:T(8,128)} %copy-done.3, f32[24,1,8,16,128]{4,0,3,2,1:T(8,128)} %copy-done.2), kind=kOutput, calls=%fused_computation.99 | convolution fusion | flops 453771264 | bytes 6300672 | tf_op jit(solution)/shard_map/dot_general | solution.py:69
  231.8 2.6 convolution_bitcast_fusion.1
  235.6 2.0 collective-permute-start.22
  237.6 1.8 collective-permute-done.22
  239.7 3.5 %collective-permute-done.23 = f32[48,48]{0,1:T(8,128)S(1)} collective-permute-done((f32[48,48]{0,1:T(8,128)S(1)}, f32[48,48]{0,1:T(8,128)S(1)}, u32[]{:S(2)}, u32[]{:S(2)}) %collective-permute-start.23) | collective-permute-done | bytes 9248 | tf_op jit(solution)/shard_map/ppermute | solution.py:113
  243.3 2.5 collective-permute-start.24
  245.8 2.2 collective-permute-done.24
  248.1 4.4 %cholesky.55 = f32[48,48]{1,0:T(8,128)S(1)} custom-call(f32[48,48]{1,0:T(8,128)S(1)} %fusion.208), custom_call_target="Cholesky" | custom-call | tf_op jit(solution)/shard_map/jit(cholesky)/cholesky | solution.py:65
  253.2 2.1 fusion.217
  255.9 3.7 %custom-call.7 = f32[1,48,48]{1,2,0:T(8,128)S(1)} custom-call(f32[1,48,48]{2,1,0:T(8,128)S(1)} %select_bitcast_fusion), custom_call_target="InvertDiagBlocksLowerTriangular" | custom-call | tf_op jit(solution)/shard_map/jit(_solve_triangular)/triangular_solve | solution.py:66
  259.8 1.6 convolution_bitcast_fusion
  261.5 1.4 copy.57
  (64 shorter events, 14.6 us)
Async XLA Ops:
  3.0 6.0 %copy-start = (f32[24,1,8,16,128]{4,3,2,1,0:T(8,128)S(1)}, f32[24,1,8,16,128]{4,3,2,1,0:T(8,128)}, u32[]{:S(2)}) copy-start(f32[24,1,8,16,128]{4,3,2,1,0:T(8,128)} %param.5) | copy-start | bytes 4718596
  3.9 25.4 %collective-permute-start.1 = (f32[24,1,8,4,128]{4,0,3,2,1:T(8,128)}, f32[24,1,8,4,128]{4,0,3,2,1:T(8,128)S(1)}, u32[]{:S(2)}, u32[]{:S(2)}) collective-permute-start(f32[24,1,8,4,128]{4,0,3,2,1:T(8,128)} %get-tuple-element.25), channel_id=1, source_target_pairs={{0,8},{2,10},{4,12},{6,14},{8,16},{10,18},{12,20},{14,22},{16,24},... | collective-permute-start | bytes 1179656 | tf_op jit(solution)/shard_map/ppermute | solution.py:38
  14.2 9.3 %collective-permute-start.2 = (f32[24,1,8,16,4]{0,3,4,2,1:T(8,128)}, f32[24,1,8,16,4]{0,3,4,2,1:T(8,128)}, u32[]{:S(2)}, u32[]{:S(2)}) collective-permute-start(f32[24,1,8,16,4]{0,3,4,2,1:T(8,128)} %copy.66), channel_id=1, source_target_pairs={{2,0},{4,2},{6,4},{10,8},{12,10},{14,12},{18,16},{20,18},{22,20},{... | collective-permute-start | bytes 147464 | tf_op jit(solution)/shard_map/ppermute | solution.py:38
  18.4 8.0 %collective-permute-start.3 = (f32[24,1,8,16,4]{0,3,4,2,1:T(8,128)}, f32[24,1,8,16,4]{0,3,4,2,1:T(8,128)}, u32[]{:S(2)}, u32[]{:S(2)}) collective-permute-start(f32[24,1,8,16,4]{0,3,4,2,1:T(8,128)} %copy.67), channel_id=1, source_target_pairs={{0,2},{2,4},{4,6},{8,10},{10,12},{12,14},{16,18},{18,20},{20,22},{... | collective-permute-start | bytes 147464 | tf_op jit(solution)/shard_map/ppermute | solution.py:38
  22.1 13.7 %collective-permute-start = (f32[24,1,8,4,128]{4,0,3,2,1:T(8,128)}, f32[24,1,8,4,128]{4,0,3,2,1:T(8,128)}, u32[]{:S(2)}, u32[]{:S(2)}) collective-permute-start(f32[24,1,8,4,128]{4,0,3,2,1:T(8,128)} %get-tuple-element.24), channel_id=1, source_target_pairs={{8,0},{10,2},{12,4},{14,6},{16,8},{18,10},{20,12},{22,14},{24,16},... | collective-permute-start | bytes 1179656 | tf_op jit(solution)/shard_map/ppermute | solution.py:38
  29.4 7.5 %copy-start.4 = (f32[24,1,8,16,4]{4,0,3,2,1:T(8,128)S(1)}, f32[24,1,8,16,4]{4,0,3,2,1:T(8,128)}, u32[]{:S(2)}) copy-start(f32[24,1,8,16,4]{4,0,3,2,1:T(8,128)} %copy.32) | copy-start | bytes 147460
  29.4 7.5 %copy-start.5 = (f32[24,1,8,16,4]{4,0,3,2,1:T(8,128)S(1)}, f32[24,1,8,16,4]{4,0,3,2,1:T(8,128)}, u32[]{:S(2)}) copy-start(f32[24,1,8,16,4]{4,0,3,2,1:T(8,128)} %copy.34) | copy-start | bytes 147460
  29.4 7.5 %copy-start.6 = (f32[1,8,16,128]{3,2,1,0:T(8,128)S(1)}, f32[1,8,16,128]{3,2,1,0:T(8,128)}, u32[]{:S(2)}) copy-start(f32[1,8,16,128]{3,2,1,0:T(8,128)} %param.6) | copy-start | bytes 196612
  44.1 9.3 %copy-start.1 = (f32[24,1,8,16,128]{4,0,3,2,1:T(8,128)}, f32[24,1,8,16,128]{4,0,3,2,1:T(8,128)S(1)}, u32[]{:S(2)}) copy-start(f32[24,1,8,16,128]{4,0,3,2,1:T(8,128)S(1)} %get-tuple-element.8) | copy-start | bytes 4718596
  45.1 21.6 %collective-permute-start.4 = (f32[24,1,8,4,128]{4,0,3,2,1:T(8,128)}, f32[24,1,8,4,128]{4,0,3,2,1:T(8,128)}, u32[]{:S(2)}, u32[]{:S(2)}) collective-permute-start(f32[24,1,8,4,128]{4,0,3,2,1:T(8,128)} %get-tuple-element.22), channel_id=1, source_target_pairs={{8,0},{10,2},{12,4},{14,6},{16,8},{18,10},{20,12},{22,14},{24,16},... | collective-permute-start | bytes 1179656 | tf_op jit(solution)/shard_map/ppermute | solution.py:38
  46.4 20.3 %collective-permute-start.5 = (f32[24,1,8,4,128]{4,0,3,2,1:T(8,128)}, f32[24,1,8,4,128]{4,0,3,2,1:T(8,128)}, u32[]{:S(2)}, u32[]{:S(2)}) collective-permute-start(f32[24,1,8,4,128]{4,0,3,2,1:T(8,128)} %get-tuple-element.23), channel_id=1, source_target_pairs={{0,8},{2,10},{4,12},{6,14},{8,16},{10,18},{12,20},{14,22},{16,24},... | collective-permute-start | bytes 1179656 | tf_op jit(solution)/shard_map/ppermute | solution.py:38
  55.7 6.1 %collective-permute-start.6 = (f32[24,1,8,16,4]{0,3,4,2,1:T(8,128)S(1)}, f32[24,1,8,16,4]{0,3,4,2,1:T(8,128)}, u32[]{:S(2)}, u32[]{:S(2)}) collective-permute-start(f32[24,1,8,16,4]{0,3,4,2,1:T(8,128)S(1)} %copy.38), channel_id=1, source_target_pairs={{2,0},{4,2},{6,4},{10,8},{12,10},{14,12},{18,16},{20,18},{22,20},{... | collective-permute-start | bytes 147464 | tf_op jit(solution)/shard_map/ppermute | solution.py:38
  58.6 6.2 %collective-permute-start.7 = (f32[24,1,8,16,4]{0,3,4,2,1:T(8,128)}, f32[24,1,8,16,4]{0,3,4,2,1:T(8,128)S(1)}, u32[]{:S(2)}, u32[]{:S(2)}) collective-permute-start(f32[24,1,8,16,4]{0,3,4,2,1:T(8,128)} %copy.40), channel_id=1, source_target_pairs={{0,2},{2,4},{4,6},{8,10},{10,12},{12,14},{16,18},{18,20},{20,22},{... | collective-permute-start | bytes 147464 | tf_op jit(solution)/shard_map/ppermute | solution.py:38
  90.6 21.5 %collective-permute-start.8 = (f32[24,1,8,4,128]{4,0,3,2,1:T(8,128)}, f32[24,1,8,4,128]{4,0,3,2,1:T(8,128)}, u32[]{:S(2)}, u32[]{:S(2)}) collective-permute-start(f32[24,1,8,4,128]{4,0,3,2,1:T(8,128)} %get-tuple-element.18), channel_id=1, source_target_pairs={{8,0},{10,2},{12,4},{14,6},{16,8},{18,10},{20,12},{22,14},{24,16},... | collective-permute-start | bytes 1179656 | tf_op jit(solution)/shard_map/ppermute | solution.py:38
  91.9 20.2 %collective-permute-start.9 = (f32[24,1,8,4,128]{4,0,3,2,1:T(8,128)}, f32[24,1,8,4,128]{4,0,3,2,1:T(8,128)}, u32[]{:S(2)}, u32[]{:S(2)}) collective-permute-start(f32[24,1,8,4,128]{4,0,3,2,1:T(8,128)} %get-tuple-element.19), channel_id=1, source_target_pairs={{0,8},{2,10},{4,12},{6,14},{8,16},{10,18},{12,20},{14,22},{16,24},... | collective-permute-start | bytes 1179656 | tf_op jit(solution)/shard_map/ppermute | solution.py:38
  101.3 6.0 %collective-permute-start.10 = (f32[24,1,8,16,4]{0,3,4,2,1:T(8,128)S(1)}, f32[24,1,8,16,4]{0,3,4,2,1:T(8,128)}, u32[]{:S(2)}, u32[]{:S(2)}) collective-permute-start(f32[24,1,8,16,4]{0,3,4,2,1:T(8,128)S(1)} %copy.43), channel_id=1, source_target_pairs={{2,0},{4,2},{6,4},{10,8},{12,10},{14,12},{18,16},{20,18},{22,20},{... | collective-permute-start | bytes 147464 | tf_op jit(solution)/shard_map/ppermute | solution.py:38
  104.2 6.0 %collective-permute-start.11 = (f32[24,1,8,16,4]{0,3,4,2,1:T(8,128)}, f32[24,1,8,16,4]{0,3,4,2,1:T(8,128)S(1)}, u32[]{:S(2)}, u32[]{:S(2)}) collective-permute-start(f32[24,1,8,16,4]{0,3,4,2,1:T(8,128)} %copy.45), channel_id=1, source_target_pairs={{0,2},{2,4},{4,6},{8,10},{10,12},{12,14},{16,18},{18,20},{20,22},{... | collective-permute-start | bytes 147464 | tf_op jit(solution)/shard_map/ppermute | solution.py:38
  123.7 27.2 %collective-permute-start.12 = (f32[24,1,8,4,128]{4,0,3,2,1:T(8,128)}, f32[24,1,8,4,128]{4,0,3,2,1:T(8,128)}, u32[]{:S(2)}, u32[]{:S(2)}) collective-permute-start(f32[24,1,8,4,128]{4,0,3,2,1:T(8,128)} %get-tuple-element.14), channel_id=1, source_target_pairs={{8,0},{10,2},{12,4},{14,6},{16,8},{18,10},{20,12},{22,14},{24,16},... | collective-permute-start | bytes 1179656 | tf_op jit(solution)/shard_map/ppermute | solution.py:38
  125.0 26.0 %collective-permute-start.13 = (f32[24,1,8,4,128]{4,0,3,2,1:T(8,128)}, f32[24,1,8,4,128]{4,0,3,2,1:T(8,128)}, u32[]{:S(2)}, u32[]{:S(2)}) collective-permute-start(f32[24,1,8,4,128]{4,0,3,2,1:T(8,128)} %get-tuple-element.15), channel_id=1, source_target_pairs={{0,8},{2,10},{4,12},{6,14},{8,16},{10,18},{12,20},{14,22},{16,24},... | collective-permute-start | bytes 1179656 | tf_op jit(solution)/shard_map/ppermute | solution.py:38
  134.8 10.3 %collective-permute-start.14 = (f32[24,1,8,16,4]{0,3,4,2,1:T(8,128)S(1)}, f32[24,1,8,16,4]{0,3,4,2,1:T(8,128)}, u32[]{:S(2)}, u32[]{:S(2)}) collective-permute-start(f32[24,1,8,16,4]{0,3,4,2,1:T(8,128)S(1)} %copy.47), channel_id=1, source_target_pairs={{2,0},{4,2},{6,4},{10,8},{12,10},{14,12},{18,16},{20,18},{22,20},{... | collective-permute-start | bytes 147464 | tf_op jit(solution)/shard_map/ppermute | solution.py:38
  139.1 8.9 %collective-permute-start.15 = (f32[24,1,8,16,4]{0,3,4,2,1:T(8,128)}, f32[24,1,8,16,4]{0,3,4,2,1:T(8,128)}, u32[]{:S(2)}, u32[]{:S(2)}) collective-permute-start(f32[24,1,8,16,4]{0,3,4,2,1:T(8,128)} %copy.49), channel_id=1, source_target_pairs={{0,2},{2,4},{4,6},{8,10},{10,12},{12,14},{16,18},{18,20},{20,22},{... | collective-permute-start | bytes 147464 | tf_op jit(solution)/shard_map/ppermute | solution.py:38
  161.9 35.7 %collective-permute-start.16 = (f32[24,1,8,16,128]{4,0,3,2,1:T(8,128)}, f32[24,1,8,16,128]{4,0,3,2,1:T(8,128)S(1)}, u32[]{:S(2)}, u32[]{:S(2)}) collective-permute-start(f32[24,1,8,16,128]{4,0,3,2,1:T(8,128)} %fusion.16), channel_id=1, source_target_pairs={{0,1},{1,0},{2,3},{3,2},{4,5},{5,4},{6,7},{7,6},{8,9},{9,8},{10,11... | collective-permute-start | bytes 4718600 | tf_op jit(solution)/shard_map/ppermute | solution.py:97
  199.3 2.6 copy-start.2
  199.3 2.6 copy-start.3
  201.9 2.6 collective-permute-start.17
  204.5 4.3 %collective-permute-start.18 = (f32[48,48]{0,1:T(8,128)S(1)}, f32[48,48]{0,1:T(8,128)S(1)}, u32[]{:S(2)}, u32[]{:S(2)}) collective-permute-start(f32[48,48]{0,1:T(8,128)S(1)} %add.444), channel_id=1, source_target_pairs={{0,4},{2,6},{4,0},{6,2},{8,12},{10,14},{12,8},{14,10},{16,20},{18,... | collective-permute-start | bytes 27656 | tf_op jit(solution)/shard_map/ppermute | solution.py:113
  208.8 3.8 %collective-permute-start.19 = (f32[48,48]{0,1:T(8,128)S(1)}, f32[48,48]{0,1:T(8,128)S(1)}, u32[]{:S(2)}, u32[]{:S(2)}) collective-permute-start(f32[48,48]{0,1:T(8,128)S(1)} %add.445), channel_id=1, source_target_pairs={{0,8},{2,10},{4,12},{6,14},{8,0},{10,2},{12,4},{14,6},{16,24},{18,... | collective-permute-start | bytes 27656 | tf_op jit(solution)/shard_map/ppermute | solution.py:113
  212.7 4.8 %collective-permute-start.20 = (f32[48,48]{0,1:T(8,128)S(1)}, f32[48,48]{0,1:T(8,128)S(1)}, u32[]{:S(2)}, u32[]{:S(2)}) collective-permute-start(f32[48,48]{0,1:T(8,128)S(1)} %add.446), channel_id=1, source_target_pairs={{0,16},{2,18},{4,20},{6,22},{8,24},{10,26},{12,28},{14,30},{16,0},... | collective-permute-start | bytes 27656 | tf_op jit(solution)/shard_map/ppermute | solution.py:113
  234.3 1.3 collective-permute-start.21
  235.6 3.8 %collective-permute-start.22 = (f32[48,48]{0,1:T(8,128)S(1)}, f32[48,48]{0,1:T(8,128)S(1)}, u32[]{:S(2)}, u32[]{:S(2)}) collective-permute-start(f32[48,48]{0,1:T(8,128)S(1)} %add.448), channel_id=1, source_target_pairs={{0,4},{2,6},{4,0},{6,2},{8,12},{10,14},{12,8},{14,10},{16,20},{18,... | collective-permute-start | bytes 27656 | tf_op jit(solution)/shard_map/ppermute | solution.py:113
  239.4 3.8 %collective-permute-start.23 = (f32[48,48]{0,1:T(8,128)S(1)}, f32[48,48]{0,1:T(8,128)S(1)}, u32[]{:S(2)}, u32[]{:S(2)}) collective-permute-start(f32[48,48]{0,1:T(8,128)S(1)} %add.449), channel_id=1, source_target_pairs={{0,8},{2,10},{4,12},{6,14},{8,0},{10,2},{12,4},{14,6},{16,24},{18,... | collective-permute-start | bytes 27656 | tf_op jit(solution)/shard_map/ppermute | solution.py:113
  243.3 4.7 %collective-permute-start.24 = (f32[48,48]{0,1:T(8,128)S(1)}, f32[48,48]{0,1:T(8,128)S(1)}, u32[]{:S(2)}, u32[]{:S(2)}) collective-permute-start(f32[48,48]{0,1:T(8,128)S(1)} %add.450), channel_id=1, source_target_pairs={{0,16},{2,18},{4,20},{6,22},{8,24},{10,26},{12,28},{14,30},{16,0},... | collective-permute-start | bytes 27656 | tf_op jit(solution)/shard_map/ppermute | solution.py:113
